TPU v7x, 512 devices: a whole 4x4x16 slice. The times are simulated.
512 devices in a mesh: member: 16 (over z), patch: 32 (over y, x, core).
Axes of the slice: x: 4, y: 4, z: 16, core: 2. Of those that a mesh axis runs over, the one named last changes fastest.
Arguments:
- ensemble: bfloat16 [16, 8192, 512], P('member', 'patch'), may hold values from -6 to 6
- forcing: bfloat16 [16, 8192, 512], P('member', 'patch'), may hold values from -6 to 6
- clone_before: int32 [16], replicated, may hold values from 0 to 15
- clone_after: int32 [16], replicated, may hold values from 0 to 15
- link_mask: int32 [64, 8], P('patch'), may hold values 0 or 1
- attn_gain: float32 [512], replicated, may hold values from 0.25 to 1.75
- w_query: bfloat16 [512, 512], replicated, may hold values from -32 to 32
- w_key: bfloat16 [512, 512], replicated, may hold values from -1 to 1
- w_value: bfloat16 [512, 512], replicated, may hold values from -0.25 to 0.25
- w_out: bfloat16 [512, 512], replicated, may hold values from -0.25 to 0.25
- mlp_gain: float32 [512], replicated, may hold values from 0.25 to 1.75
- w_up: bfloat16 [512, 1024], replicated, may hold values from -0.25 to 0.25
- w_down: bfloat16 [1024, 512], replicated, may hold values from -0.1875 to 0.1875
Outputs:
- advanced: bfloat16 [16, 8192, 512], P('member', 'patch')
All inputs are finite; a program needn't handle non-finite values. No bound on the sum of `link_mask` on one device may be relied on, other than what follows from the above.
Results may differ from a plain program's by a relative error of at most 0.006.
Values may be sent and summed in bfloat16 or wider, within the bound.
A program may use at most 64 MiB of HBM per device.

v0:
```python
import jax
import jax.numpy as jnp
from jax import lax
from jax.sharding import PartitionSpec as P

HEADS = 4
BLOCK = 128
REACH = 4


def from_behind(value, axis, steps):
    count = lax.axis_size(axis)
    pairs = [(source, (source + steps) % count) for source in range(count)]
    return lax.ppermute(value, axis, pairs)


def rms_norm(values, gain):
    scale = lax.rsqrt(jnp.mean(values * values, axis=-1, keepdims=True) + 1e-06)
    return (values * scale * gain).astype(jnp.bfloat16)


def fold_clone(states, sources):
    empty = jnp.zeros_like(states)
    pieces = lax.all_gather(states, "member", axis=0, tiled=True)
    inside = (sources >= 0) & (sources < pieces.shape[0])
    chosen = jnp.take(pieces, jnp.clip(sources, 0, pieces.shape[0] - 1), axis=0)
    return jnp.where(inside[:, None, None], chosen, empty)


def clone(states, whole_list):
    count = states.shape[0]
    here = lax.axis_index("member") * count
    sources = lax.dynamic_slice(whole_list, (here,), (count,))
    return fold_clone(states, sources)


def reach_devices(nodes):
    return REACH * BLOCK // nodes


def neighbour_normed(normed):
    reach = reach_devices(normed.shape[1])
    gathered = []
    for offset in range(-reach, reach + 1):
        if offset == 0:
            gathered.append(normed)
        else:
            gathered.append(from_behind(normed, "patch", -offset))
    return jnp.concatenate(gathered, axis=1)


def project(normed, weight):
    flat = normed.reshape(-1, normed.shape[-1])
    result = jnp.dot(flat, weight, preferred_element_type=jnp.float32).astype(jnp.bfloat16)
    return result.reshape(normed.shape[:-1] + (weight.shape[1],))


def drift(member, link_mask, attn_gain, w_query, w_key, w_value, w_out, mlp_gain, w_up, w_down):
    count, nodes, width = member.shape
    head_size = width // HEADS
    blocks = nodes // BLOCK
    reach = reach_devices(nodes)
    normed = rms_norm(member.astype(jnp.float32), attn_gain)
    queries = project(normed, w_query)
    spread_normed = neighbour_normed(normed)
    key_rows = project(spread_normed, w_key)
    value_rows = project(spread_normed, w_value)
    wide_blocks = key_rows.shape[1] // BLOCK
    key_blocks = key_rows.reshape(count, wide_blocks, BLOCK, HEADS, head_size)
    value_blocks = value_rows.reshape(count, wide_blocks, BLOCK, HEADS, head_size)
    query_blocks = queries.reshape(count, blocks, BLOCK, HEADS, head_size)
    centre = reach * blocks
    key_list = []
    value_list = []
    mask_list = []
    for offset in range(-REACH, REACH + 1):
        key_list.append(key_blocks[:, centre + offset : centre + offset + blocks])
        value_list.append(value_blocks[:, centre + offset : centre + offset + blocks])
        if offset == 0:
            allowed = jnp.ones((blocks,), dtype=bool)
        else:
            column = offset + REACH if offset < 0 else offset + REACH - 1
            allowed = link_mask[:, column] > 0
        mask_list.append(jnp.broadcast_to(allowed[:, None], (blocks, BLOCK)))
    key_cat = jnp.concatenate(key_list, axis=2)
    value_cat = jnp.concatenate(value_list, axis=2)
    allowed = jnp.concatenate(mask_list, axis=1)[None, :, None, None, :]
    scores = jnp.einsum(
        "mbqhd,mbkhd->mbhqk", query_blocks, key_cat, preferred_element_type=jnp.float32
    ) / jnp.sqrt(jnp.float32(head_size))
    scores = jnp.where(allowed, scores, -jnp.inf)
    highest = jnp.max(scores, axis=-1, keepdims=True)
    expd = jnp.exp(scores - highest)
    weights = (expd / jnp.sum(expd, axis=-1, keepdims=True)).astype(jnp.bfloat16)
    mixed = jnp.einsum(
        "mbhqk,mbkhd->mbqhd", weights, value_cat, preferred_element_type=jnp.float32
    ).astype(jnp.bfloat16)
    attended = jnp.dot(
        mixed.reshape(count * nodes, width), w_out, preferred_element_type=jnp.float32
    )
    lifted = member.reshape(count * nodes, width).astype(jnp.float32) + attended
    hidden = jax.nn.gelu(
        jnp.dot(rms_norm(lifted, mlp_gain), w_up, preferred_element_type=jnp.float32),
        approximate=True,
    ).astype(jnp.bfloat16)
    result = attended + jnp.dot(hidden, w_down, preferred_element_type=jnp.float32)
    return result.reshape(count, nodes, width).astype(jnp.bfloat16)


def shards(
    ensemble,
    forcing,
    clone_before,
    clone_after,
    link_mask,
    attn_gain,
    w_query,
    w_key,
    w_value,
    w_out,
    mlp_gain,
    w_up,
    w_down,
):
    start = clone(ensemble, clone_before)
    weights_all = (link_mask, attn_gain, w_query, w_key, w_value, w_out, mlp_gain, w_up, w_down)
    first = drift(start, *weights_all)
    noise = 0.3 * forcing.astype(jnp.float32)
    base = start.astype(jnp.float32)
    guess = (base + 0.5 * first.astype(jnp.float32) + noise).astype(jnp.bfloat16)
    second = drift(guess, *weights_all)
    total = first.astype(jnp.float32) + second.astype(jnp.float32)
    stepped = (base + 0.25 * total + noise).astype(jnp.bfloat16)
    return clone(stepped, clone_after)


def solution(mesh):
    placed = (
        P("member", "patch", None),
        P("member", "patch", None),
        P(),
        P(),
        P("patch", None),
        P(),
        P(),
        P(),
        P(),
        P(),
        P(),
        P(),
        P(),
    )
    return jax.shard_map(
        shards, mesh=mesh, in_specs=placed, out_specs=P("member", "patch", None), check_vma=False
    )
```

profile of v0, /device:TPU:6, one launch (start us, length us, event | category | flops | bytes accessed | tf_op | source)
XLA Modules:
  0.0 316.3 jit_solution(509772601200182257)
XLA Ops:
  7.3 1.2 dynamic_slice.7
  10.5 1.3 compare_reduce_fusion
  12.3 79.5 %all-gather.3.cloned.1.call-done = bf16[16,256,512]{2,1,0:T(8,128)(2,1)} async-done(((bf16[1,256,512]{2,1,0:T(8,128)(2,1)}), bf16[16,256,512]{2,1,0:T(8,128)(2,1)}) %all-gather.3.cloned.1.call-update) | async-done | bytes 4194320 | tf_op jit(solution)/shard_map/all_gather | solution.py:24
  91.8 1.1 fusion.58
  93.0 1.1 fusion.60
  94.1 3.4 %collective-permute-start = (bf16[1,256,512]{2,1,0:T(8,128)(2,1)S(1)}, bf16[1,256,512]{2,1,0:T(8,128)(2,1)S(1)}, u32[]{:S(2)}, u32[]{:S(2)}) collective-permute-start(bf16[1,256,512]{2,1,0:T(8,128)(2,1)S(1)} %fusion.60), channel_id=1, source_target_pairs={{0,2},{1,3},{2,4},{3,5},{4,6},{5,7},{6,8},{7,9},{8,10},{9,11},{10,... | collective-permute-start | bytes 786440 | tf_op jit(solution)/shard_map/ppermute | solution.py:14
  97.6 1.9 collective-permute-start.1
  99.5 3.6 %collective-permute-start.2 = (bf16[1,256,512]{2,1,0:T(8,128)(2,1)S(1)}, bf16[1,256,512]{2,1,0:T(8,128)(2,1)S(1)}, u32[]{:S(2)}, u32[]{:S(2)}) collective-permute-start(bf16[1,256,512]{2,1,0:T(8,128)(2,1)S(1)} %fusion.60), channel_id=1, source_target_pairs={{0,31},{1,0},{2,1},{3,2},{4,3},{5,4},{6,5},{7,6},{8,7},{9,8},{10,9... | collective-permute-start | bytes 786440 | tf_op jit(solution)/shard_map/ppermute | solution.py:14
  103.1 2.5 collective-permute-start.3
  105.6 1.3 convolution_convert_fusion.5
  107.0 0.8 reshape.166
  107.8 1.1 constant_dynamic-update-slice_fusion.2
  108.9 7.7 %collective-permute-done.3 = bf16[1,256,512]{2,1,0:T(8,128)(2,1)S(1)} collective-permute-done((bf16[1,256,512]{2,1,0:T(8,128)(2,1)S(1)}, bf16[1,256,512]{2,1,0:T(8,128)(2,1)S(1)}, u32[]{:S(2)}, u32[]{:S(2)}) %collective-permute-start.3) | collective-permute-done | bytes 262176 | tf_op jit(solution)/shard_map/ppermute | solution.py:14
  116.7 1.1 copy-done.10
  117.8 1.9 convolution_convert_fusion.2
  119.7 2.7 reshape_reshape.15
  122.4 1.0 fusion.120
  124.1 2.5 exponential_reduce_fusion.1
  126.6 4.1 %fusion.5 = f32[2,4,128,1152]{3,2,1,0:T(8,128)} fusion(bf16[1,2,1152,4,128]{4,2,3,1,0:T(8,128)(2,1)S(1)} %copy_dynamic-update-slice_fusion.9, pred[2,1152]{1,0:T(4,128)(4,1)S(1)} %constant_dynamic-update-slice_fusion.14, bf16[2,128,4,128]{3,2,1,0:T(4,128)(2,1)} %reshape.166), kind=kOutput, calls=%fused_computation.7 | convolution fusion | flops 304349184 | bytes 7342336 | tf_op jit(solution)/shard_map/mbqhd,mbkhd->mbhqk/dot_general | solution.py:88
  130.7 1.9 convolution_convert_fusion.3
  132.7 2.7 reshape_reshape.14
  135.3 1.8 fusion.119
  137.1 1.2 copy.132
  138.3 0.8 constant_dynamic-update-slice_fusion.13
  139.1 1.8 copy.133
  140.9 1.8 copy.134
  142.7 1.8 copy.135
  145.5 1.7 constant_dynamic-update-slice_fusion.12
  147.2 1.7 constant_dynamic-update-slice_fusion.11
  148.9 0.8 constant_dynamic-update-slice_fusion.10
  149.7 0.8 constant_dynamic-update-slice_fusion.9
  151.2 0.8 constant_dynamic-update-slice_fusion.7
  152.0 0.8 constant_dynamic-update-slice_fusion.6
  153.5 6.6 %fusion.35 = bf16[1,2,128,4,128]{2,4,3,1,0:T(8,128)(2,1)S(1)} fusion(f32[2,4,128]{2,1,0:T(4,128)S(1)} %exponential_reduce_fusion.1, bf16[1,2,1152,4,128]{2,4,3,1,0:T(8,128)(2,1)} %constant_dynamic-update-slice_fusion.5, f32[2,4,128,1152]{3,2,1,0:T(8,128)} %fusion.5), kind=kOutput, calls=%fused_computation.45 | convolution fusion | flops 305662080 | bytes 7344128 | tf_op jit(solution)/shard_map/mbhqk,mbkhd->mbqhd/dot_general | solution.py:95
  160.4 2.3 multiply_reduce_fusion.1
  162.7 3.3 %fusion.54 = (f32[256]{0:T(256)S(1)}, bf16[1,256,512]{2,1,0:T(8,128)(2,1)S(1)}, f32[256,512]{1,0:T(8,128)}) fusion(bf16[1,256,512]{2,1,0:T(8,128)(2,1)S(1)} %copy-done.17, bf16[16,256,512]{2,1,0:T(8,128)(2,1)} %all-gather.3.cloned.1.call-done, s32[]{:T(128)} %bitcast.4, pred[]{:T(512)} %bitcast.3, pred[]{:T(512)} %bitcast.2, ...), kind=kOutput, calls=%fused_computation.69 | convolution fusion | flops 542113536 | bytes 4725760 | tf_op jit(solution)/shard_map/dot_general | solution.py:106
  166.2 1.9 collective-permute-start.4
  168.2 1.9 collective-permute-start.5
  170.1 3.6 %collective-permute-start.6 = (bf16[1,256,512]{2,1,0:T(8,128)(2,1)S(1)}, bf16[1,256,512]{2,1,0:T(8,128)(2,1)S(1)}, u32[]{:S(2)}, u32[]{:S(2)}) collective-permute-start(bf16[1,256,512]{2,1,0:T(8,128)(2,1)S(1)} %fusion.56), channel_id=1, source_target_pairs={{0,31},{1,0},{2,1},{3,2},{4,3},{5,4},{6,5},{7,6},{8,7},{9,8},{10,9... | collective-permute-start | bytes 786440 | tf_op jit(solution)/shard_map/ppermute | solution.py:14
  173.7 4.1 %collective-permute-start.7 = (bf16[1,256,512]{2,1,0:T(8,128)(2,1)S(1)}, bf16[1,256,512]{2,1,0:T(8,128)(2,1)S(1)}, u32[]{:S(2)}, u32[]{:S(2)}) collective-permute-start(bf16[1,256,512]{2,1,0:T(8,128)(2,1)S(1)} %fusion.56), channel_id=1, source_target_pairs={{0,30},{1,31},{2,0},{3,1},{4,2},{5,3},{6,4},{7,5},{8,6},{9,7},{10,... | collective-permute-start | bytes 786440 | tf_op jit(solution)/shard_map/ppermute | solution.py:14
  178.2 0.8 reshape.172
  179.2 7.1 %collective-permute-done.7 = bf16[1,256,512]{2,1,0:T(8,128)(2,1)S(1)} collective-permute-done((bf16[1,256,512]{2,1,0:T(8,128)(2,1)S(1)}, bf16[1,256,512]{2,1,0:T(8,128)(2,1)S(1)}, u32[]{:S(2)}, u32[]{:S(2)}) %collective-permute-start.7) | collective-permute-done | bytes 262176 | tf_op jit(solution)/shard_map/ppermute | solution.py:14
  186.3 2.9 convolution_convert_fusion
  189.3 1.9 convolution_convert_fusion.1
  191.2 2.7 reshape_reshape.17
  193.9 1.0 fusion.118
  195.6 2.5 exponential_reduce_fusion
  198.1 3.9 %fusion.4 = f32[2,4,128,1152]{3,2,1,0:T(8,128)} fusion(bf16[1,2,1152,4,128]{4,2,3,1,0:T(8,128)(2,1)S(1)} %copy_dynamic-update-slice_fusion, pred[2,1152]{1,0:T(4,128)(4,1)S(1)} %constant_dynamic-update-slice_fusion.14, bf16[2,128,4,128]{3,2,1,0:T(4,128)(2,1)} %reshape.172), kind=kOutput, calls=%fused_computation.5 | convolution fusion | flops 304349184 | bytes 7342336 | tf_op jit(solution)/shard_map/mbqhd,mbkhd->mbhqk/dot_general | solution.py:88
  202.1 2.7 reshape_reshape.16
  204.8 1.8 fusion.117
  206.6 1.2 copy.150
  208.6 1.8 copy.151
  210.4 1.8 copy.152
  212.2 1.8 copy.153
  215.0 1.7 constant_dynamic-update-slice_fusion.35
  216.7 1.7 constant_dynamic-update-slice_fusion.34
  218.4 0.8 constant_dynamic-update-slice_fusion.33
  219.2 0.8 constant_dynamic-update-slice_fusion.32
  220.7 0.8 constant_dynamic-update-slice_fusion.30
  221.5 0.8 constant_dynamic-update-slice_fusion.29
  223.0 6.7 %fusion.32 = bf16[1,2,128,4,128]{2,4,3,1,0:T(8,128)(2,1)S(1)} fusion(f32[2,4,128]{2,1,0:T(4,128)S(1)} %exponential_reduce_fusion, bf16[1,2,1152,4,128]{2,4,3,1,0:T(8,128)(2,1)} %constant_dynamic-update-slice_fusion.28, f32[2,4,128,1152]{3,2,1,0:T(8,128)} %fusion.4), kind=kOutput, calls=%fused_computation.44 | convolution fusion | flops 305662080 | bytes 7344128 | tf_op jit(solution)/shard_map/mbhqk,mbkhd->mbqhd/dot_general | solution.py:95
  230.4 3.0 fusion.24
  235.9 71.9 %all-gather.5.cloned.1.call-done = bf16[16,256,512]{2,1,0:T(8,128)(2,1)} async-done(((bf16[1,256,512]{2,1,0:T(8,128)(2,1)}), bf16[16,256,512]{2,1,0:T(8,128)(2,1)}) %all-gather.5.cloned.1.call-update) | async-done | bytes 4194320 | tf_op jit(solution)/shard_map/all_gather | solution.py:24
  307.7 1.7 select_select_fusion
  (114 shorter events, 10.5 us)
Async XLA Ops:
  6.5 156.2 %copy-start = (bf16[1024,512]{1,0:T(8,128)(2,1)S(1)}, bf16[1024,512]{1,0:T(8,128)(2,1)}, u32[]{:S(2)}) copy-start(bf16[1024,512]{1,0:T(8,128)(2,1)} %param.27) | copy-start | bytes 3145732
  6.5 101.3 %copy-start.12 = (f32[512]{0:T(512)S(1)}, f32[512]{0:T(512)}, u32[]{:S(2)}) copy-start(f32[512]{0:T(512)} %param.20) | copy-start | bytes 6148
  6.5 85.3 %all-gather.3.cloned.1.call-start = ((), (), s32[]{:S(2)}) async-start(), calls=%async_computation | async-start | bytes 4456448 | tf_op jit(solution)/shard_map/all_gather | solution.py:24
  7.3 300.5 %all-gather.5.cloned.1.call-start = ((), (), s32[]{:S(2)}) async-start(), calls=%async_computation.1 | async-start | bytes 4456448 | tf_op jit(solution)/shard_map/all_gather | solution.py:24
  93.0 24.8 %copy-start.14 = (bf16[512,512]{1,0:T(8,128)(2,1)S(1)}, bf16[512,512]{1,0:T(8,128)(2,1)}, u32[]{:S(2)}) copy-start(bf16[512,512]{1,0:T(8,128)(2,1)} %param.22) | copy-start | bytes 1572868
  94.1 13.6 %collective-permute-start = (bf16[1,256,512]{2,1,0:T(8,128)(2,1)S(1)}, bf16[1,256,512]{2,1,0:T(8,128)(2,1)S(1)}, u32[]{:S(2)}, u32[]{:S(2)}) collective-permute-start(bf16[1,256,512]{2,1,0:T(8,128)(2,1)S(1)} %fusion.60), channel_id=1, source_target_pairs={{0,2},{1,3},{2,4},{3,5},{4,6},{5,7},{6,8},{7,9},{8,10},{9,11},{10,... | collective-permute-start | bytes 786440 | tf_op jit(solution)/shard_map/ppermute | solution.py:14
  97.6 10.2 %collective-permute-start.1 = (bf16[1,256,512]{2,1,0:T(8,128)(2,1)S(1)}, bf16[1,256,512]{2,1,0:T(8,128)(2,1)S(1)}, u32[]{:S(2)}, u32[]{:S(2)}) collective-permute-start(bf16[1,256,512]{2,1,0:T(8,128)(2,1)S(1)} %fusion.60), channel_id=1, source_target_pairs={{0,1},{1,2},{2,3},{3,4},{4,5},{5,6},{6,7},{7,8},{8,9},{9,10},{10,1... | collective-permute-start | bytes 786440 | tf_op jit(solution)/shard_map/ppermute | solution.py:14
  99.5 9.4 %collective-permute-start.2 = (bf16[1,256,512]{2,1,0:T(8,128)(2,1)S(1)}, bf16[1,256,512]{2,1,0:T(8,128)(2,1)S(1)}, u32[]{:S(2)}, u32[]{:S(2)}) collective-permute-start(bf16[1,256,512]{2,1,0:T(8,128)(2,1)S(1)} %fusion.60), channel_id=1, source_target_pairs={{0,31},{1,0},{2,1},{3,2},{4,3},{5,4},{6,5},{7,6},{8,7},{9,8},{10,9... | collective-permute-start | bytes 786440 | tf_op jit(solution)/shard_map/ppermute | solution.py:14
  103.1 13.5 %collective-permute-start.3 = (bf16[1,256,512]{2,1,0:T(8,128)(2,1)S(1)}, bf16[1,256,512]{2,1,0:T(8,128)(2,1)S(1)}, u32[]{:S(2)}, u32[]{:S(2)}) collective-permute-start(bf16[1,256,512]{2,1,0:T(8,128)(2,1)S(1)} %fusion.60), channel_id=1, source_target_pairs={{0,30},{1,31},{2,0},{3,1},{4,2},{5,3},{6,4},{7,5},{8,6},{9,7},{10,... | collective-permute-start | bytes 786440 | tf_op jit(solution)/shard_map/ppermute | solution.py:14
  116.7 1.1 copy-start.10
  126.6 4.1 %copy-start.11 = (bf16[1,1280,512]{2,1,0:T(8,128)(2,1)S(1)}, bf16[1,1280,512]{2,1,0:T(8,128)(2,1)}, u32[]{:S(2)}) copy-start(bf16[1,1280,512]{2,1,0:T(8,128)(2,1)} %copy-done.10) | copy-start | bytes 3932164
  126.6 4.1 %copy-start.15 = (bf16[512,512]{1,0:T(8,128)(2,1)S(1)}, bf16[512,512]{1,0:T(8,128)(2,1)}, u32[]{:S(2)}) copy-start(bf16[512,512]{1,0:T(8,128)(2,1)} %param.23) | copy-start | bytes 1572868
  137.1 7.3 %copy-start.4 = (bf16[1,2,128,4,128]{4,3,2,1,0:T(4,128)(2,1)S(1)}, bf16[1,2,128,4,128]{4,3,2,1,0:T(4,128)(2,1)}, u32[]{:S(2)}) copy-start(bf16[1,2,128,4,128]{4,3,2,1,0:T(4,128)(2,1)} %get-tuple-element.49) | copy-start | bytes 786436
  144.9 4.0 %copy-start.6 = (bf16[1,2,128,4,128]{2,4,3,1,0:T(8,128)(2,1)S(1)}, bf16[1,2,128,4,128]{2,4,3,1,0:T(8,128)(2,1)}, u32[]{:S(2)}) copy-start(bf16[1,2,128,4,128]{2,4,3,1,0:T(8,128)(2,1)} %copy.135) | copy-start | bytes 786436
  153.5 6.9 %copy-start.8 = (bf16[512,512]{1,0:T(8,128)(2,1)S(1)}, bf16[512,512]{1,0:T(8,128)(2,1)}, u32[]{:S(2)}) copy-start(bf16[512,512]{1,0:T(8,128)(2,1)} %param.24) | copy-start | bytes 1572868
  160.2 2.5 copy-start.13
  160.2 2.5 copy-start.17
  160.2 2.5 copy-start.19
  162.7 15.1 %copy-start.3 = (bf16[512,512]{1,0:T(8,128)(2,1)S(1)}, bf16[512,512]{1,0:T(8,128)(2,1)}, u32[]{:S(2)}) copy-start(bf16[512,512]{1,0:T(8,128)(2,1)} %param.21) | copy-start | bytes 1572868
  166.1 20.3 %copy-start.1 = (bf16[1,256,512]{2,1,0:T(8,128)(2,1)}, bf16[1,256,512]{2,1,0:T(8,128)(2,1)S(1)}, u32[]{:S(2)}) copy-start(bf16[1,256,512]{2,1,0:T(8,128)(2,1)S(1)} %get-tuple-element.26) | copy-start | bytes 786436
  166.2 12.7 %collective-permute-start.4 = (bf16[1,256,512]{2,1,0:T(8,128)(2,1)S(1)}, bf16[1,256,512]{2,1,0:T(8,128)(2,1)S(1)}, u32[]{:S(2)}, u32[]{:S(2)}) collective-permute-start(bf16[1,256,512]{2,1,0:T(8,128)(2,1)S(1)} %fusion.56), channel_id=1, source_target_pairs={{0,2},{1,3},{2,4},{3,5},{4,6},{5,7},{6,8},{7,9},{8,10},{9,11},{10,... | collective-permute-start | bytes 786440 | tf_op jit(solution)/shard_map/ppermute | solution.py:14
  168.2 10.8 %collective-permute-start.5 = (bf16[1,256,512]{2,1,0:T(8,128)(2,1)S(1)}, bf16[1,256,512]{2,1,0:T(8,128)(2,1)S(1)}, u32[]{:S(2)}, u32[]{:S(2)}) collective-permute-start(bf16[1,256,512]{2,1,0:T(8,128)(2,1)S(1)} %fusion.56), channel_id=1, source_target_pairs={{0,1},{1,2},{2,3},{3,4},{4,5},{5,6},{6,7},{7,8},{8,9},{9,10},{10,1... | collective-permute-start | bytes 786440 | tf_op jit(solution)/shard_map/ppermute | solution.py:14
  170.1 9.1 %collective-permute-start.6 = (bf16[1,256,512]{2,1,0:T(8,128)(2,1)S(1)}, bf16[1,256,512]{2,1,0:T(8,128)(2,1)S(1)}, u32[]{:S(2)}, u32[]{:S(2)}) collective-permute-start(bf16[1,256,512]{2,1,0:T(8,128)(2,1)S(1)} %fusion.56), channel_id=1, source_target_pairs={{0,31},{1,0},{2,1},{3,2},{4,3},{5,4},{6,5},{7,6},{8,7},{9,8},{10,9... | collective-permute-start | bytes 786440 | tf_op jit(solution)/shard_map/ppermute | solution.py:14
  173.7 12.6 %collective-permute-start.7 = (bf16[1,256,512]{2,1,0:T(8,128)(2,1)S(1)}, bf16[1,256,512]{2,1,0:T(8,128)(2,1)S(1)}, u32[]{:S(2)}, u32[]{:S(2)}) collective-permute-start(bf16[1,256,512]{2,1,0:T(8,128)(2,1)S(1)} %fusion.56), channel_id=1, source_target_pairs={{0,30},{1,31},{2,0},{3,1},{4,2},{5,3},{6,4},{7,5},{8,6},{9,7},{10,... | collective-permute-start | bytes 786440 | tf_op jit(solution)/shard_map/ppermute | solution.py:14
  179.1 10.2 %copy-start.16 = (bf16[512,512]{1,0:T(8,128)(2,1)S(1)}, bf16[512,512]{1,0:T(8,128)(2,1)}, u32[]{:S(2)}) copy-start(bf16[512,512]{1,0:T(8,128)(2,1)} %param.23) | copy-start | bytes 1572868
  206.6 7.4 %copy-start.5 = (bf16[1,2,128,4,128]{4,3,2,1,0:T(4,128)(2,1)S(1)}, bf16[1,2,128,4,128]{4,3,2,1,0:T(4,128)(2,1)}, u32[]{:S(2)}) copy-start(bf16[1,2,128,4,128]{4,3,2,1,0:T(4,128)(2,1)} %get-tuple-element.31) | copy-start | bytes 786436
  214.4 4.0 %copy-start.7 = (bf16[1,2,128,4,128]{2,4,3,1,0:T(8,128)(2,1)S(1)}, bf16[1,2,128,4,128]{2,4,3,1,0:T(8,128)(2,1)}, u32[]{:S(2)}) copy-start(bf16[1,2,128,4,128]{2,4,3,1,0:T(8,128)(2,1)} %copy.153) | copy-start | bytes 786436
  223.0 6.9 %copy-start.2 = (bf16[1,256,512]{2,1,0:T(8,128)(2,1)S(1)}, bf16[1,256,512]{2,1,0:T(8,128)(2,1)}, u32[]{:S(2)}) copy-start(bf16[1,256,512]{2,1,0:T(8,128)(2,1)} %copy-done.1) | copy-start | bytes 786436
  223.0 6.9 %copy-start.9 = (bf16[512,512]{1,0:T(8,128)(2,1)S(1)}, bf16[512,512]{1,0:T(8,128)(2,1)}, u32[]{:S(2)}) copy-start(bf16[512,512]{1,0:T(8,128)(2,1)} %param.24) | copy-start | bytes 1572868
  223.0 7.3 %copy-start.18 = (bf16[1,256,512]{2,1,0:T(8,128)(2,1)S(1)}, bf16[1,256,512]{2,1,0:T(8,128)(2,1)}, u32[]{:S(2)}) copy-start(bf16[1,256,512]{2,1,0:T(8,128)(2,1)} %param.16) | copy-start | bytes 786436
  223.0 7.3 %copy-start.21 = (f32[256,512]{1,0:T(8,128)S(1)}, f32[256,512]{1,0:T(8,128)}, u32[]{:S(2)}) copy-start(f32[256,512]{1,0:T(8,128)} %get-tuple-element.65) | copy-start | bytes 1572868
  230.4 3.0 copy-start.20
Sparse Core Ops, SparseCore 0:
  9.4 82.3 all-gather.2
  233.5 74.1 all-gather.4
where the time goes:
time: 318 us; the launch traced here: 316 us
  waiting for transfers between devices  167 us (53%)
  local copies, waits for them, and re-layouts  56 us (18%)
  matrix products  45.8 us (14%)
  starting transfers between devices  23 us (7%)
  between operations  17.9 us (6%)
  other arithmetic  6.56 us (2%)
    all_gather x2, waiting for transfers between devices, fold_clone(): pieces = lax.all_gather(states, 'member', axis=0, tiled=True)  151 us
    unnamed x108, local copies, waits for them, and re-layouts  34.1 us
    ppermute x8, starting transfers between devices, from_behind(): return lax.ppermute(value, axis, pairs)  23 us
    ppermute x8, waiting for transfers between devices, from_behind(): return lax.ppermute(value, axis, pairs)  14.9 us
    dot_general x2, matrix products, drift(): jnp.einsum('mbhqk,mbkhd->mbqhd', weights, value_cat, preferred_element_ty...  13.4 us
    dot_general x6, matrix products, project(): jnp.dot(flat, weight, preferred_element_type=jnp.float32)  10.4 us
    dot_general x2, matrix products, drift(): jnp.einsum('mbqhd,mbkhd->mbhqk', query_blocks, key_cat, preferred_element...  8.02 us
  transfers between devices with their start and end apart: 10, of which 4 were waited for; matrix products, arithmetic and copies ran while one was open for 3% of the time, Pallas kernels for 0%

commit v1 on v0

v1 whole, which is shorter than its diff:
```python
import functools

import jax
import jax.numpy as jnp
from jax import lax
from jax.experimental import pallas as pl
from jax.experimental.pallas import tpu as pltpu
from jax.sharding import PartitionSpec as P

HEADS = 4
BLOCK = 128
REACH = 4
CHUNKS = 4
MESH = pl.DeviceIdType.MESH
BF = jnp.bfloat16
F32 = jnp.float32


def dot(a, b):
    return jnp.dot(a, b, preferred_element_type=F32)


def dot_nt(a, b):
    return lax.dot_general(a, b, (((1,), (1,)), ((), ())), preferred_element_type=F32)


def rms(x, gain):
    scale = lax.rsqrt(jnp.mean(x * x, axis=-1, keepdims=True) + 1e-06)
    return (x * scale * gain).astype(BF)


def gelu(x):
    return 0.5 * x * (1.0 + jnp.tanh(0.7978845608028654 * (x + 0.044715 * x * x * x)))


def kernel(members, patches, *refs):
    (cb, ca, mask, e_in, f_in, g1, g2, wq_in, wk_in, wv_in, wo_in, wu_in, wd_in, out) = refs[:14]
    scratch = list(refs[14:])
    zb = [[scratch.pop(0) for _ in range(CHUNKS)] for _ in range(2)]
    nb = [scratch.pop(0) for _ in range(2)]
    wq, wk, wv, wo, wu, wd = [scratch.pop(0) for _ in range(6)]
    kb, vb, qb, mb, st, first, att, fx = [scratch.pop(0) for _ in range(8)]
    w_sem, own_sem, z_send, z_recv, h_send, h_recv = scratch

    z = lax.axis_index("member")
    p = lax.axis_index("patch")
    nodes, width = st.shape
    rows = nodes // CHUNKS
    head = width // HEADS
    right_ages = members // 2
    left_ages = members - 1 - right_ages

    def dz(off):
        return {"member": lax.rem(z + off + members, members)}

    def dp(off):
        return {"patch": lax.rem(p + off + patches, patches)}

    w_copies = [
        pltpu.make_async_copy(s, d, w_sem.at[i])
        for i, (s, d) in enumerate(zip((wq_in, wk_in, wv_in, wo_in, wu_in, wd_in), (wq, wk, wv, wo, wu, wd)))
    ]
    own = [
        [
            pltpu.make_async_copy(src.at[0, pl.ds(c * rows, rows)], zb[g][c].at[0], own_sem.at[g, c])
            for c in range(CHUNKS)
        ]
        for g, src in enumerate((e_in, f_in))
    ]
    for g in range(2):
        for c in range(CHUNKS):
            own[g][c].start()
    for w in w_copies:
        w.start()

    barrier = pltpu.get_barrier_semaphore()
    peers = [dz(1), dz(-1), dp(1), dp(-1), dp(2), dp(-2)]
    for peer in peers:
        pl.semaphore_signal(barrier, inc=1, device_id=peer, device_id_type=MESH)
    pl.semaphore_wait(barrier, len(peers))

    def ring(g, c, way, age):
        if way == 0:
            src, dst = age, age + 1
        else:
            src, dst = lax.rem(members - age, members), members - 1 - age
        return pltpu.make_async_remote_copy(
            src_ref=zb[g][c].at[src],
            dst_ref=zb[g][c].at[dst],
            send_sem=z_send.at[g, c, way],
            recv_sem=z_recv.at[g, c, way, age],
            device_id=dz(1 if way == 0 else -1),
            device_id_type=MESH,
        )

    def z_first(g):
        for c in range(CHUNKS):
            own[g][c].wait()
            ring(g, c, 0, 0).start()
            ring(g, c, 1, 0).start()

    def z_step(g, age, chunks):
        for c in chunks:
            ring(g, c, 0, age - 1).wait_recv()
            ring(g, c, 0, age).start()
            ring(g, c, 1, age - 1).wait_recv()
            ring(g, c, 1, age).start()

    def z_last(g, chunks):
        for c in chunks:
            ring(g, c, 0, right_ages - 2).wait_recv()
            ring(g, c, 0, right_ages - 1).start()
            ring(g, c, 1, left_ages - 1).wait_recv()

    def z_end(g, c):
        ring(g, c, 0, right_ages - 1).wait_recv()

    def z_drain():
        for g in range(2):
            for c in range(CHUNKS):
                for way, ages in ((0, right_ages), (1, left_ages)):
                    part = zb[g][c].at[pl.ds(0, ages)]
                    pltpu.make_async_remote_copy(
                        src_ref=part,
                        dst_ref=part,
                        send_sem=z_send.at[g, c, way],
                        recv_sem=z_recv.at[g, c, way, 0],
                        device_id=dz(1 if way == 0 else -1),
                        device_id_type=MESH,
                    ).wait_send()

    def halo(k, off, c):
        part = pl.ds(c * rows, rows)
        return pltpu.make_async_remote_copy(
            src_ref=nb[k].at[2, part],
            dst_ref=nb[k].at[2 - off, part],
            send_sem=h_send.at[k, 2 - off, c],
            recv_sem=h_recv.at[k, 2 - off, c],
            device_id=dp(off),
            device_id_type=MESH,
        )

    offsets = (1, -1, 2, -2)

    def publish(k, c, x):
        part = pl.ds(c * rows, rows)
        nb[k][2, part] = rms(x.astype(F32), g1[...])
        for off in offsets:
            halo(k, off, c).start()

    def arrive(k, slot):
        for c in range(CHUNKS):
            halo(k, 2 - slot, c).wait_recv()

    def keys_values(k, slot):
        part = pl.ds(slot * nodes, nodes)
        src = nb[k][slot]
        ks = dot(src, wk[...]).astype(BF)
        vs = dot(src, wv[...]).astype(BF)
        for h in range(HEADS):
            kb[h, part] = ks[:, h * head : (h + 1) * head]
            vb[h, part] = vs[:, h * head : (h + 1) * head]

    def queries(k):
        qs = dot(nb[k][2], wq[...]).astype(BF)
        for h in range(HEADS):
            qb[h] = qs[:, h * head : (h + 1) * head]

    factor = 1.4426950408889634 / head**0.5
    span = 2 * REACH + 1

    def attend(b, h):
        kv = pl.ds(b * BLOCK, span * BLOCK)
        s = dot_nt(qb[h, pl.ds(b * BLOCK, BLOCK)], kb[h, kv]) * factor
        parts = []
        for i in range(span):
            piece = s[:, i * BLOCK : (i + 1) * BLOCK]
            if i != REACH:
                link = mask[b, i if i < REACH else i - 1]
                piece = piece + jnp.where(link > 0, F32(0.0), F32(-jnp.inf))
            parts.append(piece)
        s = jnp.concatenate(parts, axis=1)
        top = jnp.max(s, axis=1, keepdims=True)
        e = jnp.exp2(s - top)
        total = jnp.sum(e, axis=1, keepdims=True)
        mixed = dot(e.astype(BF), vb[h, kv]) / total
        mb[pl.ds(b * BLOCK, BLOCK), pl.ds(pl.multiple_of(h * head, head), head)] = mixed.astype(BF)

    def finish(state):
        att[...] = dot(mb[...], wo[...])
        lifted = state[...].astype(F32) + att[...]
        hidden = gelu(dot(rms(lifted, g2[...]), wu[...])).astype(BF)
        return (att[...] + dot(hidden, wd[...])).astype(BF)

    z_first(0)

    @pl.loop(1, left_ages)
    def _(age):
        z_step(0, age, range(CHUNKS))

    z_last(0, range(CHUNKS))
    z_first(1)

    d_e = lax.rem(z - cb[ca[z]] + members, members)
    d_f = lax.rem(z - ca[z] + members, members)
    for c in range(CHUNKS):
        z_end(0, c)
        part = pl.ds(c * rows, rows)
        x = zb[0][c][d_e]
        st[part] = x
        publish(0, c, x)
    for w in w_copies:
        w.wait()
    queries(0)
    keys_values(0, 2)
    z_step(1, 1, range(CHUNKS))
    for slot in (1, 3):
        arrive(0, slot)
        keys_values(0, slot)
    z_step(1, 2, range(CHUNKS))
    for slot in (0, 4):
        arrive(0, slot)
        keys_values(0, slot)

    half = CHUNKS // 2

    @pl.loop(0, HEADS)
    def _(h):
        attend(0, h)

        @pl.when(h < HEADS - 1)
        def _():
            z_step(1, 3 + h, range(half))

        attend(1, h)

        @pl.when(h < HEADS - 1)
        def _():
            z_step(1, 3 + h, range(half, CHUNKS))

    first[...] = finish(st)

    @pl.loop(3 + HEADS - 1, left_ages)
    def _(age):
        z_step(1, age, range(CHUNKS))

    z_last(1, range(CHUNKS))
    for c in range(CHUNKS):
        z_end(1, c)
        part = pl.ds(c * rows, rows)
        base = st[part].astype(F32) + 0.3 * zb[1][c][d_f].astype(F32)
        x = (base + 0.5 * first[part].astype(F32)).astype(BF)
        fx[part] = x
        publish(1, c, x)
    queries(1)
    keys_values(1, 2)
    for slot in (1, 3, 0, 4):
        arrive(1, slot)
        keys_values(1, slot)

    @pl.loop(0, HEADS)
    def _(h):
        attend(0, h)
        attend(1, h)

    second = finish(fx).astype(F32)
    for c in range(CHUNKS):
        part = pl.ds(c * rows, rows)
        base = st[part].astype(F32)
        tot = first[part].astype(F32) + second[c * rows : (c + 1) * rows]
        out[0, part] = (base + 0.25 * tot + 0.3 * zb[1][c][d_f].astype(F32)).astype(BF)

    for k in range(2):
        for off in offsets:
            for c in range(CHUNKS):
                halo(k, off, c).wait_send()
    z_drain()


def solution(mesh):
    members, patches = mesh.shape["member"], mesh.shape["patch"]

    def shards(ensemble, forcing, cb, ca, mask, g1, wq, wk, wv, wo, g2, wu, wd):
        _, nodes, width = ensemble.shape
        hidden = wu.shape[1]
        rows = nodes // CHUNKS
        head = width // HEADS
        smem = pl.BlockSpec(memory_space=pltpu.SMEM)
        vmem = pl.BlockSpec(memory_space=pltpu.VMEM)
        anym = pl.BlockSpec(memory_space=pl.ANY)
        return pl.pallas_call(
            functools.partial(kernel, members, patches),
            out_shape=jax.ShapeDtypeStruct(ensemble.shape, BF),
            in_specs=[smem] * 3 + [anym] * 2 + [vmem] * 2 + [anym] * 6,
            out_specs=vmem,
            scratch_shapes=[pltpu.VMEM((members, rows, width), BF) for _ in range(2 * CHUNKS)]
            + [pltpu.VMEM((5, nodes, width), BF) for _ in range(2)]
            + [pltpu.VMEM((width, width), BF) for _ in range(4)]
            + [pltpu.VMEM((width, hidden), BF), pltpu.VMEM((hidden, width), BF)]
            + [
                pltpu.VMEM((HEADS, 5 * nodes, head), BF),
                pltpu.VMEM((HEADS, 5 * nodes, head), BF),
                pltpu.VMEM((HEADS, nodes, head), BF),
                pltpu.VMEM((nodes, width), BF),
                pltpu.VMEM((nodes, width), BF),
                pltpu.VMEM((nodes, width), BF),
                pltpu.VMEM((nodes, width), F32),
                pltpu.VMEM((nodes, width), BF),
                pltpu.SemaphoreType.DMA((6,)),
                pltpu.SemaphoreType.DMA((2, CHUNKS)),
                pltpu.SemaphoreType.DMA((2, CHUNKS, 2)),
                pltpu.SemaphoreType.DMA((2, CHUNKS, 2, members // 2)),
                pltpu.SemaphoreType.DMA((2, 5, CHUNKS)),
                pltpu.SemaphoreType.DMA((2, 5, CHUNKS)),
            ],
            compiler_params=pltpu.CompilerParams(
                collective_id=0, has_side_effects=True, vmem_limit_bytes=56 * 1024 * 1024
            ),
            name="heun",
        )(cb, ca, mask, ensemble, forcing, g1.reshape(1, width), g2.reshape(1, width), wq, wk, wv, wo, wu, wd)

    placed = (P("member", "patch", None),) * 2 + (P(), P(), P("patch", None)) + (P(),) * 8
    return jax.shard_map(
        shards, mesh=mesh, in_specs=placed, out_specs=P("member", "patch", None), check_vma=False
    )
```

time: 318 us -> 124 us (0.39)
  the two profiles are of different devices: /device:TPU:6 before, /device:TPU:1 now
where the time goes in v1:
time: 124 us
  Pallas kernels  122 us (98%)
  local copies, waits for them, and re-layouts  1.67 us (1%)
    pallas_call x1, Pallas kernels, shards(): pl.pallas_call(functools.partial(kernel, members, patches), out_shape=jax...  122 us

profile of v1, /device:TPU:1, one launch (start us, length us, event | category | flops | bytes accessed | tf_op | source)
XLA Modules:
  0.0 124.2 jit_solution(4176133223769978465)
XLA Ops:
  0.0 122.5 %heun.1 = bf16[1,256,512]{2,1,0:T(8,128)(2,1)} custom-call(s32[16]{0:T(128)} %refs_0_.1, s32[16]{0:T(128)} %refs_1_.1, s32[2,8]{1,0:T(2,128)} %refs_2_.1, bf16[1,256,512]{2,1,0:T(8,128)(2,1)} %refs_3_.1, bf16[1,256,512]{2,1,0:T(8,128)(2,1)} %refs_4_.1, f32[1,512]{1,0:T(1,128)} %bitcast.2, f32[1,512]{1,0:T(1,128)} %bitcast.3, bf16[512,512]{1,0:T(8,128)(2,1)} %refs_7_.1, ...), custom_call_target="tpu_custom_call" | custom-call | tf_op jit(solution)/shard_map/heun/pallas_call | solution.py:291
  122.5 1.7 %copy.15 = bf16[1,256,512]{2,1,0:T(8,128)(2,1)} copy(bf16[1,256,512]{2,1,0:T(8,128)(2,1)} %heun.1) | data formatting | bytes 524288

commit v2 on v1

--- a/solution.py
+++ b/solution.py
@@ -11,6 +11,12 @@
 BLOCK = 128
 REACH = 4
 CHUNKS = 4
+PIECES = 8
+LAG = 4
+HOPS = 10
+PLANS = 64
+MID = 48
+STEPS = 72
 MESH = pl.DeviceIdType.MESH
 BF = jnp.bfloat16
 F32 = jnp.float32
@@ -33,7 +39,86 @@
     return 0.5 * x * (1.0 + jnp.tanh(0.7978845608028654 * (x + 0.044715 * x * x * x)))
 
 
-def kernel(members, patches, *refs):
+def drift_tools(
+    chunks, p, dp, mask, g1, g2, nb, wq, wk, wv, wo, wu, wd, kb, vb, qb, mb, att, h_send, h_recv
+):
+    _, nodes, width = nb[0].shape
+    rows = nodes // chunks
+    head = width // HEADS
+
+    def halo(k, off, c):
+        part = pl.ds(c * rows, rows)
+        return pltpu.make_async_remote_copy(
+            src_ref=nb[k].at[2, part],
+            dst_ref=nb[k].at[2 - off, part],
+            send_sem=h_send.at[k, 2 - off, c],
+            recv_sem=h_recv.at[k, 2 - off, c],
+            device_id=dp(off),
+            device_id_type=MESH,
+        )
+
+    offsets = (1, -1, 2, -2)
+
+    def publish(k, c, x):
+        part = pl.ds(c * rows, rows)
+        nb[k][2, part] = rms(x.astype(F32), g1[...])
+        for off in offsets:
+            halo(k, off, c).start()
+
+    def arrive(k, slot):
+        for c in range(chunks):
+            halo(k, 2 - slot, c).wait_recv()
+
+    def keys_values(k, slot):
+        part = pl.ds(slot * nodes, nodes)
+        src = nb[k][slot]
+        ks = dot(src, wk[...]).astype(BF)
+        vs = dot(src, wv[...]).astype(BF)
+        for h in range(HEADS):
+            kb[h, part] = ks[:, h * head : (h + 1) * head]
+            vb[h, part] = vs[:, h * head : (h + 1) * head]
+
+    def queries(k):
+        qs = dot(nb[k][2], wq[...]).astype(BF)
+        for h in range(HEADS):
+            qb[h] = qs[:, h * head : (h + 1) * head]
+
+    factor = 1.4426950408889634 / head**0.5
+    span = 2 * REACH + 1
+
+    def attend(b, h):
+        kv = pl.ds(b * BLOCK, span * BLOCK)
+        s = dot_nt(qb[h, pl.ds(b * BLOCK, BLOCK)], kb[h, kv]) * factor
+        parts = []
+        for i in range(span):
+            piece = s[:, i * BLOCK : (i + 1) * BLOCK]
+            if i != REACH:
+                link = mask[b, i if i < REACH else i - 1]
+                piece = piece + jnp.where(link > 0, F32(0.0), F32(-jnp.inf))
+            parts.append(piece)
+        s = jnp.concatenate(parts, axis=1)
+        top = jnp.max(s, axis=1, keepdims=True)
+        e = jnp.exp2(s - top)
+        total = jnp.sum(e, axis=1, keepdims=True)
+        mixed = dot(e.astype(BF), vb[h, kv]) / total
+        mb[pl.ds(b * BLOCK, BLOCK), pl.ds(pl.multiple_of(h * head, head), head)] = mixed.astype(BF)
+
+    def finish(state):
+        att[...] = dot(mb[...], wo[...])
+        lifted = state[...].astype(F32) + att[...]
+        hidden = gelu(dot(rms(lifted, g2[...]), wu[...])).astype(BF)
+        return (att[...] + dot(hidden, wd[...])).astype(BF)
+
+    def h_drain():
+        for k in range(2):
+            for off in offsets:
+                for c in range(chunks):
+                    halo(k, off, c).wait_send()
+
+    return publish, arrive, keys_values, queries, attend, finish, h_drain
+
+
+def ring_kernel(members, patches, *refs):
     (cb, ca, mask, e_in, f_in, g1, g2, wq_in, wk_in, wv_in, wo_in, wu_in, wd_in, out) = refs[:14]
     scratch = list(refs[14:])
     zb = [[scratch.pop(0) for _ in range(CHUNKS)] for _ in range(2)]
@@ -129,68 +214,9 @@
                         device_id_type=MESH,
                     ).wait_send()
 
-    def halo(k, off, c):
-        part = pl.ds(c * rows, rows)
-        return pltpu.make_async_remote_copy(
-            src_ref=nb[k].at[2, part],
-            dst_ref=nb[k].at[2 - off, part],
-            send_sem=h_send.at[k, 2 - off, c],
-            recv_sem=h_recv.at[k, 2 - off, c],
-            device_id=dp(off),
-            device_id_type=MESH,
-        )
-
-    offsets = (1, -1, 2, -2)
-
-    def publish(k, c, x):
-        part = pl.ds(c * rows, rows)
-        nb[k][2, part] = rms(x.astype(F32), g1[...])
-        for off in offsets:
-            halo(k, off, c).start()
-
-    def arrive(k, slot):
-        for c in range(CHUNKS):
-            halo(k, 2 - slot, c).wait_recv()
-
-    def keys_values(k, slot):
-        part = pl.ds(slot * nodes, nodes)
-        src = nb[k][slot]
-        ks = dot(src, wk[...]).astype(BF)
-        vs = dot(src, wv[...]).astype(BF)
-        for h in range(HEADS):
-            kb[h, part] = ks[:, h * head : (h + 1) * head]
-            vb[h, part] = vs[:, h * head : (h + 1) * head]
-
-    def queries(k):
-        qs = dot(nb[k][2], wq[...]).astype(BF)
-        for h in range(HEADS):
-            qb[h] = qs[:, h * head : (h + 1) * head]
-
-    factor = 1.4426950408889634 / head**0.5
-    span = 2 * REACH + 1
-
-    def attend(b, h):
-        kv = pl.ds(b * BLOCK, span * BLOCK)
-        s = dot_nt(qb[h, pl.ds(b * BLOCK, BLOCK)], kb[h, kv]) * factor
-        parts = []
-        for i in range(span):
-            piece = s[:, i * BLOCK : (i + 1) * BLOCK]
-            if i != REACH:
-                link = mask[b, i if i < REACH else i - 1]
-                piece = piece + jnp.where(link > 0, F32(0.0), F32(-jnp.inf))
-            parts.append(piece)
-        s = jnp.concatenate(parts, axis=1)
-        top = jnp.max(s, axis=1, keepdims=True)
-        e = jnp.exp2(s - top)
-        total = jnp.sum(e, axis=1, keepdims=True)
-        mixed = dot(e.astype(BF), vb[h, kv]) / total
-        mb[pl.ds(b * BLOCK, BLOCK), pl.ds(pl.multiple_of(h * head, head), head)] = mixed.astype(BF)
-
-    def finish(state):
-        att[...] = dot(mb[...], wo[...])
-        lifted = state[...].astype(F32) + att[...]
-        hidden = gelu(dot(rms(lifted, g2[...]), wu[...])).astype(BF)
-        return (att[...] + dot(hidden, wd[...])).astype(BF)
+    publish, arrive, keys_values, queries, attend, finish, h_drain = drift_tools(
+        CHUNKS, p, dp, mask, g1, g2, nb, wq, wk, wv, wo, wu, wd, kb, vb, qb, mb, att, h_send, h_recv
+    )
 
     z_first(0)
 
@@ -270,11 +296,271 @@
         tot = first[part].astype(F32) + second[c * rows : (c + 1) * rows]
         out[0, part] = (base + 0.25 * tot + 0.3 * zb[1][c][d_f].astype(F32)).astype(BF)
 
-    for k in range(2):
-        for off in offsets:
-            for c in range(CHUNKS):
-                halo(k, off, c).wait_send()
+    h_drain()
     z_drain()
+
+
+def thresholds(shape, members, g):
+    q = lax.broadcasted_iota(jnp.int32, shape, 0)
+    s = lax.rem(lax.broadcasted_iota(jnp.int32, shape, 1), members)
+    x = (q * 40503 + s * 30011 + (g * 12289 + 7)) & 0xFFFF
+    x = (x * 25173 + 13849) & 0xFFFF
+    x = x ^ (x >> 7)
+    x = (x * 25173 + 13849) & 0xFFFF
+    x = x ^ (x >> 9)
+    half = members // 2
+    low = members - HOPS
+    wide = low + ((x * (HOPS - low + 1)) >> 16)
+    near = half - 1 + ((x * 2) >> 16)
+    return jnp.where(q == 0, half, jnp.where(q == 1, half - 1, jnp.where(q < shape[0] // 4, near, wide)))
+
+
+def make_plan(members, z, sources, starts, plan):
+    shape = starts.shape[2:]
+    lane = lax.broadcasted_iota(jnp.int32, shape, 1)
+    slot = lax.rem(lane, members)
+    zero = jnp.zeros(shape, jnp.int32)
+    reach = []
+    for g in range(2):
+        src = zero
+        for m in range(members):
+            src = jnp.where(slot == m, sources[g][m], src)
+        dist = lax.rem(slot - src + members, members)
+        right = dist <= thresholds(shape, members, g)
+        away = (jnp.where(right, dist, 0), jnp.where(right, 0, members - dist))
+        both = []
+        for way in range(2):
+            far = zero
+            for b in range(1, HOPS + 1):
+                shift = (128 - b) if way == 0 else b
+                far = jnp.where(pltpu.roll(away[way], shift, 1) == b, b, far)
+            both.append(far)
+        reach.append(both)
+    free = [zero, zero]
+    ends = []
+    for g in range(2):
+        before = [None, None]
+        for a in range(HOPS):
+            for way in range(2):
+                sgn = 1 if way == 0 else 127
+                far = reach[g][way]
+                if a > 0:
+                    far = pltpu.roll(far, a if way == 0 else 128 - a, 1)
+                need = far > a
+                t = free[way]
+                if a > 0:
+                    t = jnp.maximum(t, pltpu.roll(before[way], sgn, 1) + LAG)
+                free[way] = jnp.where(need, t + PIECES, free[way])
+                before[way] = jnp.where(need, t, -4096)
+                starts[way, g * HOPS + a] = before[way]
+        ends.append(jnp.max(jnp.maximum(free[0], free[1]), axis=1, keepdims=True))
+    late = jnp.maximum(ends[0] - MID, ends[1] - STEPS)
+    late = jnp.broadcast_to(late, shape)
+    key = late * PLANS + lax.broadcasted_iota(jnp.int32, shape, 0)
+    best = jnp.min(key, axis=0, keepdims=True)
+    picked = key == best
+    fits = jnp.where(best < PLANS, 1, 0)
+
+    items = 2 * HOPS
+    lane1 = lax.broadcasted_iota(jnp.int32, (1, 128), 1)
+    sent, came = [], []
+    for way in range(2):
+        from_lane = lax.rem(z + members - 1, members) if way == 0 else lax.rem(z + 1, members)
+        mine, theirs = [], []
+        for r in range(items):
+            row = jnp.sum(jnp.where(picked, starts[way, r], 0), axis=0, keepdims=True)
+            mine.append(jnp.broadcast_to(jnp.sum(jnp.where(lane1 == z, row, 0), axis=1, keepdims=True), (1, 128)))
+            theirs.append(
+                jnp.broadcast_to(jnp.sum(jnp.where(lane1 == from_lane, row, 0), axis=1, keepdims=True), (1, 128))
+            )
+        sent.append(mine)
+        came.append(theirs)
+    top = 2 * PIECES + 2 * STEPS
+    rows = []
+    for way in range(2):
+        base = 2 * PIECES + way * STEPS
+        index = jnp.zeros((1, 128), jnp.int32)
+        for g in range(2):
+            for a in range(HOPS):
+                at = sent[way][g * HOPS + a]
+                first = g * PIECES if a == 0 else base + came[way][g * HOPS + a - 1]
+                hit = (lane1 >= at) & (lane1 < at + PIECES)
+                index = jnp.where(hit, first + lane1 - at, index)
+        rows.append(jnp.clip(index, 0, top - 1))
+    return rows, came, fits, lane1, top
+
+
+def route_kernel(members, patches, *refs):
+    (cb, ca, mask, e_in, f_in, g1, g2, wq_in, wk_in, wv_in, wo_in, wu_in, wd_in, out, fine) = refs[:15]
+    scratch = list(refs[15:])
+    nb = [scratch.pop(0) for _ in range(2)]
+    wq, wk, wv, wo, wu, wd = [scratch.pop(0) for _ in range(6)]
+    kb, vb, qb, mb, st, first, att, fx = [scratch.pop(0) for _ in range(8)]
+    pool, staged, landed, starts, plan, table = [scratch.pop(0) for _ in range(6)]
+    w_sem, own_sem, plan_sem, z_send, z_recv, h_send, h_recv = scratch
+
+    z = lax.axis_index("member")
+    p = lax.axis_index("patch")
+    nodes, width = st.shape
+    rows = nodes // PIECES
+
+    def dz(off):
+        return {"member": lax.rem(z + off + members, members)}
+
+    def dp(off):
+        return {"patch": lax.rem(p + off + patches, patches)}
+
+    own = [
+        pltpu.make_async_copy(src.at[0, pl.ds(c * rows, rows)], pool.at[g * PIECES + c], own_sem.at[g, c])
+        for g, src in enumerate((e_in, f_in))
+        for c in range(PIECES)
+    ]
+    for copy in own:
+        copy.start()
+    w_copies = [
+        pltpu.make_async_copy(s, d, w_sem.at[i])
+        for i, (s, d) in enumerate(zip((wq_in, wk_in, wv_in, wo_in, wu_in, wd_in), (wq, wk, wv, wo, wu, wd)))
+    ]
+    for w in w_copies:
+        w.start()
+    barrier = pltpu.get_barrier_semaphore()
+    peers = [dz(1), dz(-1), dp(1), dp(-1), dp(2), dp(-2)]
+    for peer in peers:
+        pl.semaphore_signal(barrier, inc=1, device_id=peer, device_id_type=MESH)
+
+    moved = [ca[s] for s in range(members)]
+    sources = ([cb[m] for m in moved], moved)
+    index, came, fits, lane1, top = make_plan(members, z, sources, starts, plan)
+    mine = ca[z]
+    finals = []
+    for g, src in enumerate((cb[mine], mine)):
+        dist = lax.rem(z - src + members, members)
+        at = jnp.full((1, 128), g * PIECES, jnp.int32)
+        for way in (1, 0):
+            gone = dist if way == 0 else members - dist
+            for a in range(HOPS):
+                begin = came[way][g * HOPS + a]
+                use = (begin >= 0) & (gone == a + 1)
+                at = jnp.where(use, 2 * PIECES + way * STEPS + begin, at)
+        finals.append(jnp.clip(at, 0, top - PIECES))
+    plan[...] = jnp.zeros(plan.shape, jnp.int32)
+    for r, row in enumerate((index[0], index[1], finals[0], finals[1], fits)):
+        plan[pl.ds(r, 1)] = row
+    to_smem = pltpu.make_async_copy(plan, table, plan_sem)
+    to_smem.start()
+    for copy in own:
+        copy.wait()
+    pl.semaphore_wait(barrier, len(peers))
+    to_smem.wait()
+    fine[0, 0] = table[4, 0]
+
+    def hop(way, t):
+        return pltpu.make_async_remote_copy(
+            src_ref=staged.at[way, t],
+            dst_ref=landed.at[way, t],
+            send_sem=z_send.at[way],
+            recv_sem=z_recv.at[way, t],
+            device_id=dz(1 if way == 0 else -1),
+            device_id_type=MESH,
+        )
+
+    def take(t):
+        for way in range(2):
+            hop(way, t).wait_recv()
+            pool[2 * PIECES + way * STEPS + t] = landed[way, t]
+
+    def give(t):
+        for way in range(2):
+            staged[way, t] = pool[table[way, t]]
+            hop(way, t).start()
+
+    def step(t):
+        take(t - LAG)
+        give(t)
+
+    def piece(g, c):
+        return pool[table[2 + g, 0] + c]
+
+    publish, arrive, keys_values, queries, attend, finish, h_drain = drift_tools(
+        PIECES, p, dp, mask, g1, g2, nb, wq, wk, wv, wo, wu, wd, kb, vb, qb, mb, att, h_send, h_recv
+    )
+
+    for t in range(LAG):
+        give(t)
+
+    @pl.loop(LAG, MID - PIECES + LAG)
+    def _(t):
+        step(t)
+
+    for c in range(PIECES):
+        step(MID - PIECES + LAG + c)
+        x = piece(0, c)
+        st[pl.ds(c * rows, rows)] = x
+        publish(0, c, x)
+    for w in w_copies:
+        w.wait()
+    now = MID + LAG
+    queries(0)
+    step(now)
+    keys_values(0, 2)
+    for t in range(now + 1, now + 6):
+        step(t)
+    now += 6
+    for slot, count in ((1, 1), (3, 2), (0, 1), (4, 1)):
+        arrive(0, slot)
+        keys_values(0, slot)
+        for t in range(now, now + count):
+            step(t)
+        now += count
+
+    @pl.loop(0, HEADS)
+    def _(h):
+        attend(0, h)
+        step(now + 2 * h)
+        attend(1, h)
+        step(now + 2 * h + 1)
+
+    now += 2 * HEADS
+    for t in range(now, STEPS):
+        step(t)
+    first[...] = finish(st)
+    for c in range(PIECES):
+        t = STEPS - PIECES + c
+        if t >= STEPS - LAG:
+            take(t)
+        part = pl.ds(c * rows, rows)
+        base = st[part].astype(F32) + 0.3 * piece(1, c).astype(F32)
+        x = (base + 0.5 * first[part].astype(F32)).astype(BF)
+        fx[part] = x
+        publish(1, c, x)
+    queries(1)
+    keys_values(1, 2)
+    for slot in (1, 3, 0, 4):
+        arrive(1, slot)
+        keys_values(1, slot)
+
+    @pl.loop(0, HEADS)
+    def _(h):
+        attend(0, h)
+        attend(1, h)
+
+    second = finish(fx).astype(F32)
+    for c in range(PIECES):
+        part = pl.ds(c * rows, rows)
+        base = st[part].astype(F32)
+        tot = first[part].astype(F32) + second[c * rows : (c + 1) * rows]
+        out[0, part] = (base + 0.25 * tot + 0.3 * piece(1, c).astype(F32)).astype(BF)
+
+    h_drain()
+    for way in range(2):
+        pltpu.make_async_remote_copy(
+            src_ref=staged.at[way],
+            dst_ref=landed.at[way],
+            send_sem=z_send.at[way],
+            recv_sem=z_recv.at[way, 0],
+            device_id=dz(1 if way == 0 else -1),
+            device_id_type=MESH,
+        ).wait_send()
 
 
 def solution(mesh):
@@ -288,36 +574,72 @@
         smem = pl.BlockSpec(memory_space=pltpu.SMEM)
         vmem = pl.BlockSpec(memory_space=pltpu.VMEM)
         anym = pl.BlockSpec(memory_space=pl.ANY)
-        return pl.pallas_call(
-            functools.partial(kernel, members, patches),
-            out_shape=jax.ShapeDtypeStruct(ensemble.shape, BF),
-            in_specs=[smem] * 3 + [anym] * 2 + [vmem] * 2 + [anym] * 6,
-            out_specs=vmem,
-            scratch_shapes=[pltpu.VMEM((members, rows, width), BF) for _ in range(2 * CHUNKS)]
-            + [pltpu.VMEM((5, nodes, width), BF) for _ in range(2)]
+        state = jax.ShapeDtypeStruct(ensemble.shape, BF)
+        common = (
+            [pltpu.VMEM((5, nodes, width), BF) for _ in range(2)]
             + [pltpu.VMEM((width, width), BF) for _ in range(4)]
             + [pltpu.VMEM((width, hidden), BF), pltpu.VMEM((hidden, width), BF)]
+            + [pltpu.VMEM((HEADS, 5 * nodes, head), BF) for _ in range(2)]
+            + [pltpu.VMEM((HEADS, nodes, head), BF)]
+            + [pltpu.VMEM((nodes, width), BF) for _ in range(3)]
+            + [pltpu.VMEM((nodes, width), F32), pltpu.VMEM((nodes, width), BF)]
+        )
+        dma = pltpu.SemaphoreType.DMA
+
+        def params(cid):
+            return pltpu.CompilerParams(
+                collective_id=cid, has_side_effects=True, vmem_limit_bytes=56 * 1024 * 1024
+            )
+
+        ins = [smem] * 3 + [anym] * 2 + [vmem] * 2 + [anym] * 6
+        args = (cb, ca, mask, ensemble, forcing, g1.reshape(1, width), g2.reshape(1, width), wq, wk, wv, wo, wu, wd)
+        size = nodes // PIECES
+        out, fine = pl.pallas_call(
+            functools.partial(route_kernel, members, patches),
+            out_shape=(state, jax.ShapeDtypeStruct((1, 1), jnp.int32)),
+            in_specs=ins,
+            out_specs=(vmem, smem),
+            scratch_shapes=common
             + [
-                pltpu.VMEM((HEADS, 5 * nodes, head), BF),
-                pltpu.VMEM((HEADS, 5 * nodes, head), BF),
-                pltpu.VMEM((HEADS, nodes, head), BF),
-                pltpu.VMEM((nodes, width), BF),
-                pltpu.VMEM((nodes, width), BF),
-                pltpu.VMEM((nodes, width), BF),
-                pltpu.VMEM((nodes, width), F32),
-                pltpu.VMEM((nodes, width), BF),
-                pltpu.SemaphoreType.DMA((6,)),
-                pltpu.SemaphoreType.DMA((2, CHUNKS)),
-                pltpu.SemaphoreType.DMA((2, CHUNKS, 2)),
-                pltpu.SemaphoreType.DMA((2, CHUNKS, 2, members // 2)),
-                pltpu.SemaphoreType.DMA((2, 5, CHUNKS)),
-                pltpu.SemaphoreType.DMA((2, 5, CHUNKS)),
+                pltpu.VMEM((2 * PIECES + 2 * STEPS, size, width), BF),
+                pltpu.VMEM((2, STEPS, size, width), BF),
+                pltpu.VMEM((2, STEPS, size, width), BF),
+                pltpu.VMEM((2, 2 * HOPS, PLANS, 128), jnp.int32),
+                pltpu.VMEM((8, 128), jnp.int32),
+                pltpu.SMEM((8, 128), jnp.int32),
+                dma((6,)),
+                dma((2, PIECES)),
+                dma,
+                dma((2,)),
+                dma((2, STEPS)),
+                dma((2, 5, PIECES)),
+                dma((2, 5, PIECES)),
             ],
-            compiler_params=pltpu.CompilerParams(
-                collective_id=0, has_side_effects=True, vmem_limit_bytes=56 * 1024 * 1024
-            ),
-            name="heun",
-        )(cb, ca, mask, ensemble, forcing, g1.reshape(1, width), g2.reshape(1, width), wq, wk, wv, wo, wu, wd)
+            compiler_params=params(0),
+            name="route",
+        )(*args)
+
+        def slow(_):
+            return pl.pallas_call(
+                functools.partial(ring_kernel, members, patches),
+                out_shape=state,
+                in_specs=ins,
+                out_specs=vmem,
+                scratch_shapes=[pltpu.VMEM((members, rows, width), BF) for _ in range(2 * CHUNKS)]
+                + common
+                + [
+                    dma((6,)),
+                    dma((2, CHUNKS)),
+                    dma((2, CHUNKS, 2)),
+                    dma((2, CHUNKS, 2, members // 2)),
+                    dma((2, 5, CHUNKS)),
+                    dma((2, 5, CHUNKS)),
+                ],
+                compiler_params=params(1),
+                name="ring",
+            )(*args)
+
+        return lax.cond(fine[0, 0] > 0, lambda x: x, slow, out)
 
     placed = (P("member", "patch", None),) * 2 + (P(), P(), P("patch", None)) + (P(),) * 8
     return jax.shard_map(

time: 124 us -> 102 us (0.82)
  Pallas kernels: 122 us -> 99.3 us
    pallas_call x1, Pallas kernels: 122 us -> 99.3 us  [shards(): pl.pallas_call(functools.partial(route_kernel, members, patches), out_sha...]
where the time goes in v2:
time: 102 us
  Pallas kernels  99.3 us (97%)
  local copies, waits for them, and re-layouts  2 us (2%)
    pallas_call x1, Pallas kernels, shards(): pl.pallas_call(functools.partial(route_kernel, members, patches), out_sha...  99.3 us

profile of v2, /device:TPU:1, one launch (start us, length us, event | category | flops | bytes accessed | tf_op | source)
XLA Modules:
  0.0 102.0 jit_solution(11826246338077813460)
XLA Ops:
  0.0 0.0 copy-start.9
  0.0 0.0 copy-start.8
  0.0 0.0 copy-start.10
  0.0 0.0 copy-start.11
  0.0 0.7 copy-done.9
  0.7 0.0 copy-done.8
  0.7 0.0 copy-done.10
  0.7 0.0 copy-done.11
  0.7 0.0 copy-start
  0.7 0.0 copy-start.1
  0.7 0.0 copy-start.2
  0.7 0.0 copy-start.3
  0.7 0.0 copy-start.4
  0.7 0.0 copy-start.5
  0.8 0.0 copy-start.6
  0.8 0.0 copy-start.7
  0.8 99.3 %route.1 = (bf16[1,256,512]{2,1,0:T(8,128)(2,1)S(1)}, s32[1,1]{1,0:T(1,128)}) custom-call(s32[16]{0:T(128)S(1)} %copy-done.11, s32[16]{0:T(128)} %refs_1_.1, s32[2,8]{1,0:T(2,128)S(1)} %copy-done.10, bf16[1,256,512]{2,1,0:T(8,128)(2,1)} %refs_3_.1, bf16[1,256,512]{2,1,0:T(8,128)(2,1)} %refs_4_.1, f32[1,512]{1,0:T(1,128)S(1)} %bitcast.3, ...), custom_call_target="tpu_custom_call" | custom-call | tf_op jit(solution)/shard_map/route/pallas_call | solution.py:597
  100.7 0.0 copy-start.12
  100.7 0.0 copy-done
  100.7 0.0 copy-done.1
  100.7 0.0 copy-done.2
  100.7 0.0 copy-done.3
  100.7 0.0 copy-done.4
  100.7 0.0 copy-done.5
  100.7 0.0 copy-done.6
  100.7 0.0 copy-done.7
  100.8 0.6 copy-done.12
  101.3 0.7 copy.19
  (1 shorter events, 0.0 us)
Async XLA Ops:
  0.0 0.7 copy-start.9
  0.0 0.7 copy-start.8
  0.0 0.7 copy-start.10
  0.0 0.7 copy-start.11
  0.7 100.0 %copy-start = (bf16[512,1024]{1,0:T(8,128)(2,1)S(1)}, bf16[512,1024]{1,0:T(8,128)(2,1)}, u32[]{:S(2)}) copy-start(bf16[512,1024]{1,0:T(8,128)(2,1)} %refs_11_.1) | copy-start | bytes 3145732
  0.7 100.0 %copy-start.1 = (bf16[1024,512]{1,0:T(8,128)(2,1)S(1)}, bf16[1024,512]{1,0:T(8,128)(2,1)}, u32[]{:S(2)}) copy-start(bf16[1024,512]{1,0:T(8,128)(2,1)} %refs_12_.1) | copy-start | bytes 3145732
  0.7 100.0 %copy-start.2 = (bf16[512,512]{1,0:T(8,128)(2,1)S(1)}, bf16[512,512]{1,0:T(8,128)(2,1)}, u32[]{:S(2)}) copy-start(bf16[512,512]{1,0:T(8,128)(2,1)} %refs_7_.1) | copy-start | bytes 1572868
  0.7 100.0 %copy-start.3 = (bf16[512,512]{1,0:T(8,128)(2,1)S(1)}, bf16[512,512]{1,0:T(8,128)(2,1)}, u32[]{:S(2)}) copy-start(bf16[512,512]{1,0:T(8,128)(2,1)} %refs_8_.1) | copy-start | bytes 1572868
  0.7 100.0 %copy-start.4 = (bf16[512,512]{1,0:T(8,128)(2,1)S(1)}, bf16[512,512]{1,0:T(8,128)(2,1)}, u32[]{:S(2)}) copy-start(bf16[512,512]{1,0:T(8,128)(2,1)} %refs_9_.1) | copy-start | bytes 1572868
  0.7 100.0 %copy-start.5 = (bf16[512,512]{1,0:T(8,128)(2,1)S(1)}, bf16[512,512]{1,0:T(8,128)(2,1)}, u32[]{:S(2)}) copy-start(bf16[512,512]{1,0:T(8,128)(2,1)} %refs_10_.1) | copy-start | bytes 1572868
  0.8 100.0 %copy-start.6 = (bf16[1,256,512]{2,1,0:T(8,128)(2,1)S(1)}, bf16[1,256,512]{2,1,0:T(8,128)(2,1)}, u32[]{:S(2)}) copy-start(bf16[1,256,512]{2,1,0:T(8,128)(2,1)} %refs_3_.1) | copy-start | bytes 786436
  0.8 100.0 %copy-start.7 = (bf16[1,256,512]{2,1,0:T(8,128)(2,1)S(1)}, bf16[1,256,512]{2,1,0:T(8,128)(2,1)}, u32[]{:S(2)}) copy-start(bf16[1,256,512]{2,1,0:T(8,128)(2,1)} %refs_4_.1) | copy-start | bytes 786436
  100.7 0.7 copy-start.12

commit v3 on v2

--- a/solution.py
+++ b/solution.py
@@ -12,11 +12,12 @@
 REACH = 4
 CHUNKS = 4
 PIECES = 8
-LAG = 4
+LAG = 5
 HOPS = 10
 PLANS = 64
-MID = 48
-STEPS = 72
+MID = 55
+STEPS = 73
+BEHIND = 3
 MESH = pl.DeviceIdType.MESH
 BF = jnp.bfloat16
 F32 = jnp.float32
@@ -337,23 +338,23 @@
             both.append(far)
         reach.append(both)
     free = [zero, zero]
-    ends = []
-    for g in range(2):
-        before = [None, None]
-        for a in range(HOPS):
-            for way in range(2):
-                sgn = 1 if way == 0 else 127
-                far = reach[g][way]
-                if a > 0:
-                    far = pltpu.roll(far, a if way == 0 else 128 - a, 1)
-                need = far > a
-                t = free[way]
-                if a > 0:
-                    t = jnp.maximum(t, pltpu.roll(before[way], sgn, 1) + LAG)
-                free[way] = jnp.where(need, t + PIECES, free[way])
-                before[way] = jnp.where(need, t, -4096)
-                starts[way, g * HOPS + a] = before[way]
-        ends.append(jnp.max(jnp.maximum(free[0], free[1]), axis=1, keepdims=True))
+    ends = [zero, zero]
+    before = [[None, None], [None, None]]
+    for g, a in sorted(((g, a) for g in range(2) for a in range(HOPS)), key=lambda hop: (hop[1] + BEHIND * hop[0], hop[0])):
+        for way in range(2):
+            sgn = 1 if way == 0 else 127
+            far = reach[g][way]
+            if a > 0:
+                far = pltpu.roll(far, a if way == 0 else 128 - a, 1)
+            need = far > a
+            t = free[way]
+            if a > 0:
+                t = jnp.maximum(t, pltpu.roll(before[g][way], sgn, 1) + LAG)
+            free[way] = jnp.where(need, t + PIECES, free[way])
+            ends[g] = jnp.maximum(ends[g], jnp.where(need, t + PIECES, 0))
+            before[g][way] = jnp.where(need, t, -4096)
+            starts[way, g * HOPS + a] = before[g][way]
+    ends = [jnp.max(end, axis=1, keepdims=True) for end in ends]
     late = jnp.maximum(ends[0] - MID, ends[1] - STEPS)
     late = jnp.broadcast_to(late, shape)
     key = late * PLANS + lax.broadcasted_iota(jnp.int32, shape, 0)
@@ -464,19 +465,18 @@
             device_id_type=MESH,
         )
 
-    def take(t):
+    def take(t, way):
+        hop(way, t).wait_recv()
+        pool[2 * PIECES + way * STEPS + t] = landed[way, t]
+
+    def give(t, way):
+        staged[way, t] = pool[table[way, t]]
+        hop(way, t).start()
+
+    def step(t):
         for way in range(2):
-            hop(way, t).wait_recv()
-            pool[2 * PIECES + way * STEPS + t] = landed[way, t]
-
-    def give(t):
-        for way in range(2):
-            staged[way, t] = pool[table[way, t]]
-            hop(way, t).start()
-
-    def step(t):
-        take(t - LAG)
-        give(t)
+            take(t - LAG, way)
+            give(t, way)
 
     def piece(g, c):
         return pool[table[2 + g, 0] + c]
@@ -486,7 +486,8 @@
     )
 
     for t in range(LAG):
-        give(t)
+        for way in range(2):
+            give(t, way)
 
     @pl.loop(LAG, MID - PIECES + LAG)
     def _(t):
@@ -503,31 +504,29 @@
     queries(0)
     step(now)
     keys_values(0, 2)
-    for t in range(now + 1, now + 6):
+    for t in range(now + 1, now + 7):
         step(t)
-    now += 6
-    for slot, count in ((1, 1), (3, 2), (0, 1), (4, 1)):
+    now += 7
+    for slot, count in ((1, 1), (3, 1), (0, 2), (4, 2)):
         arrive(0, slot)
         keys_values(0, slot)
         for t in range(now, now + count):
             step(t)
         now += count
+    for t in range(now, STEPS):
+        step(t)
 
     @pl.loop(0, HEADS)
     def _(h):
         attend(0, h)
-        step(now + 2 * h)
         attend(1, h)
-        step(now + 2 * h + 1)
-
-    now += 2 * HEADS
-    for t in range(now, STEPS):
-        step(t)
+
     first[...] = finish(st)
     for c in range(PIECES):
         t = STEPS - PIECES + c
         if t >= STEPS - LAG:
-            take(t)
+            for way in range(2):
+                take(t, way)
         part = pl.ds(c * rows, rows)
         base = st[part].astype(F32) + 0.3 * piece(1, c).astype(F32)
         x = (base + 0.5 * first[part].astype(F32)).astype(BF)

time: 102 us -> 94 us (0.922)
  Pallas kernels: 99.3 us -> 91.1 us
    pallas_call x1, Pallas kernels: 99.3 us -> 91.1 us  [shards(): pl.pallas_call(functools.partial(route_kernel, members, patches), out_sha...]
where the time goes in v3:
time: 94 us; the launch traced here: 93.9 us
  Pallas kernels  91.1 us (97%)
  local copies, waits for them, and re-layouts  2 us (2%)
    pallas_call x1, Pallas kernels, shards(): pl.pallas_call(functools.partial(route_kernel, members, patches), out_sha...  91.1 us
    unnamed x27, local copies, waits for them, and re-layouts  2 us

profile of v3, /device:TPU:1, one launch (start us, length us, event | category | flops | bytes accessed | tf_op | source)
XLA Modules:
  0.0 93.9 jit_solution(10994207830088740851)
XLA Ops:
  0.0 0.0 copy-start.9
  0.0 0.0 copy-start.8
  0.0 0.0 copy-start.10
  0.0 0.0 copy-start.11
  0.0 0.7 copy-done.9
  0.7 0.0 copy-done.8
  0.7 0.0 copy-done.10
  0.7 0.0 copy-done.11
  0.7 0.0 copy-start
  0.7 0.0 copy-start.1
  0.7 0.0 copy-start.2
  0.7 0.0 copy-start.3
  0.7 0.0 copy-start.4
  0.7 0.0 copy-start.5
  0.8 0.0 copy-start.6
  0.8 0.0 copy-start.7
  0.8 91.1 %route.1 = (bf16[1,256,512]{2,1,0:T(8,128)(2,1)S(1)}, s32[1,1]{1,0:T(1,128)}) custom-call(s32[16]{0:T(128)S(1)} %copy-done.11, s32[16]{0:T(128)} %refs_1_.1, s32[2,8]{1,0:T(2,128)S(1)} %copy-done.10, bf16[1,256,512]{2,1,0:T(8,128)(2,1)} %refs_3_.1, bf16[1,256,512]{2,1,0:T(8,128)(2,1)} %refs_4_.1, f32[1,512]{1,0:T(1,128)S(1)} %bitcast.3, ...), custom_call_target="tpu_custom_call" | custom-call | tf_op jit(solution)/shard_map/route/pallas_call | solution.py:596
  92.5 0.0 copy-start.12
  92.5 0.0 copy-done
  92.6 0.0 copy-done.1
  92.6 0.0 copy-done.2
  92.6 0.0 copy-done.3
  92.6 0.0 copy-done.4
  92.6 0.0 copy-done.5
  92.6 0.0 copy-done.6
  92.6 0.0 copy-done.7
  92.6 0.6 copy-done.12
  93.2 0.7 copy.19
  (1 shorter events, 0.0 us)
Async XLA Ops:
  0.0 0.7 copy-start.9
  0.0 0.7 copy-start.8
  0.0 0.7 copy-start.10
  0.0 0.7 copy-start.11
  0.7 91.8 %copy-start = (bf16[512,1024]{1,0:T(8,128)(2,1)S(1)}, bf16[512,1024]{1,0:T(8,128)(2,1)}, u32[]{:S(2)}) copy-start(bf16[512,1024]{1,0:T(8,128)(2,1)} %refs_11_.1) | copy-start | bytes 3145732
  0.7 91.8 %copy-start.1 = (bf16[1024,512]{1,0:T(8,128)(2,1)S(1)}, bf16[1024,512]{1,0:T(8,128)(2,1)}, u32[]{:S(2)}) copy-start(bf16[1024,512]{1,0:T(8,128)(2,1)} %refs_12_.1) | copy-start | bytes 3145732
  0.7 91.9 %copy-start.2 = (bf16[512,512]{1,0:T(8,128)(2,1)S(1)}, bf16[512,512]{1,0:T(8,128)(2,1)}, u32[]{:S(2)}) copy-start(bf16[512,512]{1,0:T(8,128)(2,1)} %refs_7_.1) | copy-start | bytes 1572868
  0.7 91.9 %copy-start.3 = (bf16[512,512]{1,0:T(8,128)(2,1)S(1)}, bf16[512,512]{1,0:T(8,128)(2,1)}, u32[]{:S(2)}) copy-start(bf16[512,512]{1,0:T(8,128)(2,1)} %refs_8_.1) | copy-start | bytes 1572868
  0.7 91.9 %copy-start.4 = (bf16[512,512]{1,0:T(8,128)(2,1)S(1)}, bf16[512,512]{1,0:T(8,128)(2,1)}, u32[]{:S(2)}) copy-start(bf16[512,512]{1,0:T(8,128)(2,1)} %refs_9_.1) | copy-start | bytes 1572868
  0.7 91.9 %copy-start.5 = (bf16[512,512]{1,0:T(8,128)(2,1)S(1)}, bf16[512,512]{1,0:T(8,128)(2,1)}, u32[]{:S(2)}) copy-start(bf16[512,512]{1,0:T(8,128)(2,1)} %refs_10_.1) | copy-start | bytes 1572868
  0.8 91.9 %copy-start.6 = (bf16[1,256,512]{2,1,0:T(8,128)(2,1)S(1)}, bf16[1,256,512]{2,1,0:T(8,128)(2,1)}, u32[]{:S(2)}) copy-start(bf16[1,256,512]{2,1,0:T(8,128)(2,1)} %refs_3_.1) | copy-start | bytes 786436
  0.8 91.9 %copy-start.7 = (bf16[1,256,512]{2,1,0:T(8,128)(2,1)S(1)}, bf16[1,256,512]{2,1,0:T(8,128)(2,1)}, u32[]{:S(2)}) copy-start(bf16[1,256,512]{2,1,0:T(8,128)(2,1)} %refs_4_.1) | copy-start | bytes 786436
  92.5 0.7 copy-start.12

commit v4 on v3

--- a/solution.py
+++ b/solution.py
@@ -47,37 +47,52 @@
     rows = nodes // chunks
     head = width // HEADS
 
-    def halo(k, off, c):
+    side = 2 * lax.rem(p, 2) - 1
+    partner, outer, same, last = 2 - side, 2 + side, 2 + 2 * side, 2 - 2 * side
+
+    def copy_rows(k, c, src, dst, off, sem):
         part = pl.ds(c * rows, rows)
         return pltpu.make_async_remote_copy(
-            src_ref=nb[k].at[2, part],
-            dst_ref=nb[k].at[2 - off, part],
-            send_sem=h_send.at[k, 2 - off, c],
-            recv_sem=h_recv.at[k, 2 - off, c],
+            src_ref=nb[k].at[src, part],
+            dst_ref=nb[k].at[dst, part],
+            send_sem=h_send.at[k, sem, c],
+            recv_sem=h_recv.at[k, dst, c],
             device_id=dp(off),
             device_id_type=MESH,
         )
 
-    offsets = (1, -1, 2, -2)
+    def sends(k, c):
+        return (
+            copy_rows(k, c, 2, partner, side, 1),
+            copy_rows(k, c, 2, same, -2 * side, 2),
+            copy_rows(k, c, 2, outer, -side, 0),
+        )
+
+    def hand_on(k, c):
+        return copy_rows(k, c, outer, same, -side, 3)
 
     def publish(k, c, x):
         part = pl.ds(c * rows, rows)
         nb[k][2, part] = rms(x.astype(F32), g1[...])
-        for off in offsets:
-            halo(k, off, c).start()
+        for send in sends(k, c):
+            send.start()
+
+    def relay(k, c):
+        copy_rows(k, c, 2, outer, side, 0).wait_recv()
+        hand_on(k, c).start()
 
     def arrive(k, slot):
         for c in range(chunks):
-            halo(k, 2 - slot, c).wait_recv()
+            copy_rows(k, c, 2, slot, side, 0).wait_recv()
 
     def keys_values(k, slot):
-        part = pl.ds(slot * nodes, nodes)
+        part = pl.ds(pl.multiple_of(slot * nodes, nodes), nodes)
         src = nb[k][slot]
         ks = dot(src, wk[...]).astype(BF)
         vs = dot(src, wv[...]).astype(BF)
         for h in range(HEADS):
             kb[h, part] = ks[:, h * head : (h + 1) * head]
-            vb[h, part] = vs[:, h * head : (h + 1) * head]
+            vb[h, part, pl.ds(0, head)] = vs[:, h * head : (h + 1) * head]
 
     def queries(k):
         qs = dot(nb[k][2], wq[...]).astype(BF)
@@ -101,8 +116,27 @@
         top = jnp.max(s, axis=1, keepdims=True)
         e = jnp.exp2(s - top)
         total = jnp.sum(e, axis=1, keepdims=True)
-        mixed = dot(e.astype(BF), vb[h, kv]) / total
+        mixed = dot(e.astype(BF), vb[h, kv, pl.ds(0, head)]) / total
         mb[pl.ds(b * BLOCK, BLOCK), pl.ds(pl.multiple_of(h * head, head), head)] = mixed.astype(BF)
+
+    def attend_all(h):
+        s = dot_nt(qb[h], kb[h]) * factor
+        probs = []
+        for b in range(nodes // BLOCK):
+            parts = []
+            for i in range(span):
+                piece = s[b * BLOCK : (b + 1) * BLOCK, (b + i) * BLOCK : (b + i + 1) * BLOCK]
+                if i != REACH:
+                    link = mask[b, i if i < REACH else i - 1]
+                    piece = piece + jnp.where(link > 0, F32(0.0), F32(-jnp.inf))
+                parts.append(piece)
+            sb = jnp.concatenate(parts, axis=1)
+            e = jnp.exp2(sb - jnp.max(sb, axis=1, keepdims=True)).astype(BF)
+            blank = jnp.zeros((BLOCK, BLOCK), BF)
+            probs.append(jnp.concatenate([blank] * b + [e] + [blank] * (nodes // BLOCK - 1 - b), axis=1))
+        both = dot(jnp.concatenate(probs, axis=0), vb[h])
+        mixed = both[:, :head] / both[:, head:]
+        mb[:, pl.ds(pl.multiple_of(h * head, head), head)] = mixed.astype(BF)
 
     def finish(state):
         att[...] = dot(mb[...], wo[...])
@@ -112,11 +146,11 @@
 
     def h_drain():
         for k in range(2):
-            for off in offsets:
-                for c in range(chunks):
-                    halo(k, off, c).wait_send()
-
-    return publish, arrive, keys_values, queries, attend, finish, h_drain
+            for c in range(chunks):
+                for send in sends(k, c) + (hand_on(k, c),):
+                    send.wait_send()
+
+    return (partner, outer, same, last), publish, relay, arrive, keys_values, queries, attend, attend_all, finish, h_drain
 
 
 def ring_kernel(members, patches, *refs):
@@ -215,7 +249,7 @@
                         device_id_type=MESH,
                     ).wait_send()
 
-    publish, arrive, keys_values, queries, attend, finish, h_drain = drift_tools(
+    slots, publish, relay, arrive, keys_values, queries, attend, _, finish, h_drain = drift_tools(
         CHUNKS, p, dp, mask, g1, g2, nb, wq, wk, wv, wo, wu, wd, kb, vb, qb, mb, att, h_send, h_recv
     )
 
@@ -241,11 +275,14 @@
     queries(0)
     keys_values(0, 2)
     z_step(1, 1, range(CHUNKS))
-    for slot in (1, 3):
-        arrive(0, slot)
-        keys_values(0, slot)
+    partner, outer, same, last = slots
+    for c in range(CHUNKS):
+        relay(0, c)
+    arrive(0, partner)
+    keys_values(0, partner)
+    keys_values(0, outer)
     z_step(1, 2, range(CHUNKS))
-    for slot in (0, 4):
+    for slot in (same, last):
         arrive(0, slot)
         keys_values(0, slot)
 
@@ -281,7 +318,12 @@
         publish(1, c, x)
     queries(1)
     keys_values(1, 2)
-    for slot in (1, 3, 0, 4):
+    for c in range(CHUNKS):
+        relay(1, c)
+    arrive(1, partner)
+    keys_values(1, partner)
+    keys_values(1, outer)
+    for slot in (same, last):
         arrive(1, slot)
         keys_values(1, slot)
 
@@ -449,6 +491,8 @@
         plan[pl.ds(r, 1)] = row
     to_smem = pltpu.make_async_copy(plan, table, plan_sem)
     to_smem.start()
+    for h in range(HEADS):
+        vb[h, :, pl.ds(width // HEADS, width // HEADS)] = jnp.ones((vb.shape[1], width // HEADS), BF)
     for copy in own:
         copy.wait()
     pl.semaphore_wait(barrier, len(peers))
@@ -481,7 +525,7 @@
     def piece(g, c):
         return pool[table[2 + g, 0] + c]
 
-    publish, arrive, keys_values, queries, attend, finish, h_drain = drift_tools(
+    slots, publish, relay, arrive, keys_values, queries, _, attend_all, finish, h_drain = drift_tools(
         PIECES, p, dp, mask, g1, g2, nb, wq, wk, wv, wo, wu, wd, kb, vb, qb, mb, att, h_send, h_recv
     )
 
@@ -493,21 +537,35 @@
     def _(t):
         step(t)
 
+    partner, outer, same, last = slots
+    delay = 5
     for c in range(PIECES):
         step(MID - PIECES + LAG + c)
         x = piece(0, c)
         st[pl.ds(c * rows, rows)] = x
         publish(0, c, x)
+        if c >= delay:
+            relay(0, c - delay)
     for w in w_copies:
         w.wait()
     now = MID + LAG
     queries(0)
     step(now)
+    relay(0, PIECES - delay)
     keys_values(0, 2)
-    for t in range(now + 1, now + 7):
-        step(t)
-    now += 7
-    for slot, count in ((1, 1), (3, 1), (0, 2), (4, 2)):
+    step(now + 1)
+    relay(0, PIECES - delay + 1)
+    arrive(0, partner)
+    step(now + 2)
+    relay(0, PIECES - delay + 2)
+    keys_values(0, partner)
+    step(now + 3)
+    relay(0, PIECES - delay + 3)
+    step(now + 4)
+    relay(0, PIECES - delay + 4)
+    keys_values(0, outer)
+    now += 5
+    for slot, count in ((same, 2), (last, 2)):
         arrive(0, slot)
         keys_values(0, slot)
         for t in range(now, now + count):
@@ -516,10 +574,8 @@
     for t in range(now, STEPS):
         step(t)
 
-    @pl.loop(0, HEADS)
-    def _(h):
-        attend(0, h)
-        attend(1, h)
+    for h in range(HEADS):
+        attend_all(h)
 
     first[...] = finish(st)
     for c in range(PIECES):
@@ -534,14 +590,19 @@
         publish(1, c, x)
     queries(1)
     keys_values(1, 2)
-    for slot in (1, 3, 0, 4):
+    for c in range(PIECES // 2):
+        relay(1, c)
+    arrive(1, partner)
+    keys_values(1, partner)
+    for c in range(PIECES // 2, PIECES):
+        relay(1, c)
+    keys_values(1, outer)
+    for slot in (same, last):
         arrive(1, slot)
         keys_values(1, slot)
 
-    @pl.loop(0, HEADS)
-    def _(h):
-        attend(0, h)
-        attend(1, h)
+    for h in range(HEADS):
+        attend_all(h)
 
     second = finish(fx).astype(F32)
     for c in range(PIECES):
@@ -578,7 +639,7 @@
             [pltpu.VMEM((5, nodes, width), BF) for _ in range(2)]
             + [pltpu.VMEM((width, width), BF) for _ in range(4)]
             + [pltpu.VMEM((width, hidden), BF), pltpu.VMEM((hidden, width), BF)]
-            + [pltpu.VMEM((HEADS, 5 * nodes, head), BF) for _ in range(2)]
+            + [pltpu.VMEM((HEADS, 5 * nodes, head), BF), pltpu.VMEM((HEADS, 5 * nodes, 2 * head), BF)]
             + [pltpu.VMEM((HEADS, nodes, head), BF)]
             + [pltpu.VMEM((nodes, width), BF) for _ in range(3)]
             + [pltpu.VMEM((nodes, width), F32), pltpu.VMEM((nodes, width), BF)]

time: 94 us -> 90.7 us (0.965)
  Pallas kernels: 91.1 us -> 87.8 us
    pallas_call x1, Pallas kernels: 91.1 us -> 87.8 us  [shards(): pl.pallas_call(functools.partial(route_kernel, members, patches), out_sha...]
where the time goes in v4:
time: 90.7 us; the launch traced here: 90.6 us
  Pallas kernels  87.8 us (97%)
  local copies, waits for them, and re-layouts  2 us (2%)
    pallas_call x1, Pallas kernels, shards(): pl.pallas_call(functools.partial(route_kernel, members, patches), out_sha...  87.8 us
    unnamed x27, local copies, waits for them, and re-layouts  2 us

profile of v4, /device:TPU:1, one launch (start us, length us, event | category | flops | bytes accessed | tf_op | source)
XLA Modules:
  0.0 90.6 jit_solution(6144729533825295520)
XLA Ops:
  0.0 0.0 copy-start.9
  0.0 0.0 copy-start.8
  0.0 0.0 copy-start.10
  0.0 0.0 copy-start.11
  0.0 0.7 copy-done.9
  0.7 0.0 copy-done.8
  0.7 0.0 copy-done.10
  0.7 0.0 copy-done.11
  0.7 0.0 copy-start
  0.7 0.0 copy-start.1
  0.7 0.0 copy-start.2
  0.7 0.0 copy-start.3
  0.7 0.0 copy-start.4
  0.7 0.0 copy-start.5
  0.8 0.0 copy-start.6
  0.8 0.0 copy-start.7
  0.8 87.8 %route.1 = (bf16[1,256,512]{2,1,0:T(8,128)(2,1)S(1)}, s32[1,1]{1,0:T(1,128)}) custom-call(s32[16]{0:T(128)S(1)} %copy-done.11, s32[16]{0:T(128)} %refs_1_.1, s32[2,8]{1,0:T(2,128)S(1)} %copy-done.10, bf16[1,256,512]{2,1,0:T(8,128)(2,1)} %refs_3_.1, bf16[1,256,512]{2,1,0:T(8,128)(2,1)} %refs_4_.1, f32[1,512]{1,0:T(1,128)S(1)} %bitcast.3, ...), custom_call_target="tpu_custom_call" | custom-call | tf_op jit(solution)/shard_map/route/pallas_call | solution.py:657
  89.2 0.0 copy-start.12
  89.2 0.0 copy-done
  89.2 0.0 copy-done.1
  89.3 0.0 copy-done.2
  89.3 0.0 copy-done.3
  89.3 0.0 copy-done.4
  89.3 0.0 copy-done.5
  89.3 0.0 copy-done.6
  89.3 0.0 copy-done.7
  89.3 0.6 copy-done.12
  89.9 0.7 copy.19
  (1 shorter events, 0.0 us)
Async XLA Ops:
  0.0 0.7 copy-start.9
  0.0 0.7 copy-start.8
  0.0 0.7 copy-start.10
  0.0 0.7 copy-start.11
  0.7 88.5 %copy-start = (bf16[512,1024]{1,0:T(8,128)(2,1)S(1)}, bf16[512,1024]{1,0:T(8,128)(2,1)}, u32[]{:S(2)}) copy-start(bf16[512,1024]{1,0:T(8,128)(2,1)} %refs_11_.1) | copy-start | bytes 3145732
  0.7 88.5 %copy-start.1 = (bf16[1024,512]{1,0:T(8,128)(2,1)S(1)}, bf16[1024,512]{1,0:T(8,128)(2,1)}, u32[]{:S(2)}) copy-start(bf16[1024,512]{1,0:T(8,128)(2,1)} %refs_12_.1) | copy-start | bytes 3145732
  0.7 88.5 %copy-start.2 = (bf16[512,512]{1,0:T(8,128)(2,1)S(1)}, bf16[512,512]{1,0:T(8,128)(2,1)}, u32[]{:S(2)}) copy-start(bf16[512,512]{1,0:T(8,128)(2,1)} %refs_7_.1) | copy-start | bytes 1572868
  0.7 88.5 %copy-start.3 = (bf16[512,512]{1,0:T(8,128)(2,1)S(1)}, bf16[512,512]{1,0:T(8,128)(2,1)}, u32[]{:S(2)}) copy-start(bf16[512,512]{1,0:T(8,128)(2,1)} %refs_8_.1) | copy-start | bytes 1572868
  0.7 88.5 %copy-start.4 = (bf16[512,512]{1,0:T(8,128)(2,1)S(1)}, bf16[512,512]{1,0:T(8,128)(2,1)}, u32[]{:S(2)}) copy-start(bf16[512,512]{1,0:T(8,128)(2,1)} %refs_9_.1) | copy-start | bytes 1572868
  0.7 88.5 %copy-start.5 = (bf16[512,512]{1,0:T(8,128)(2,1)S(1)}, bf16[512,512]{1,0:T(8,128)(2,1)}, u32[]{:S(2)}) copy-start(bf16[512,512]{1,0:T(8,128)(2,1)} %refs_10_.1) | copy-start | bytes 1572868
  0.8 88.5 %copy-start.6 = (bf16[1,256,512]{2,1,0:T(8,128)(2,1)S(1)}, bf16[1,256,512]{2,1,0:T(8,128)(2,1)}, u32[]{:S(2)}) copy-start(bf16[1,256,512]{2,1,0:T(8,128)(2,1)} %refs_3_.1) | copy-start | bytes 786436
  0.8 88.5 %copy-start.7 = (bf16[1,256,512]{2,1,0:T(8,128)(2,1)S(1)}, bf16[1,256,512]{2,1,0:T(8,128)(2,1)}, u32[]{:S(2)}) copy-start(bf16[1,256,512]{2,1,0:T(8,128)(2,1)} %refs_4_.1) | copy-start | bytes 786436
  89.2 0.7 copy-start.12

commit v5 on v4

--- a/solution.py
+++ b/solution.py
@@ -138,11 +138,11 @@
         mixed = both[:, :head] / both[:, head:]
         mb[:, pl.ds(pl.multiple_of(h * head, head), head)] = mixed.astype(BF)
 
-    def finish(state):
-        att[...] = dot(mb[...], wo[...])
-        lifted = state[...].astype(F32) + att[...]
+    def finish(state, part=slice(None)):
+        att[part] = dot(mb[part], wo[...])
+        lifted = state[part].astype(F32) + att[part]
         hidden = gelu(dot(rms(lifted, g2[...]), wu[...])).astype(BF)
-        return (att[...] + dot(hidden, wd[...])).astype(BF)
+        return (att[part] + dot(hidden, wd[...])).astype(BF)
 
     def h_drain():
         for k in range(2):
@@ -525,7 +525,7 @@
     def piece(g, c):
         return pool[table[2 + g, 0] + c]
 
-    slots, publish, relay, arrive, keys_values, queries, _, attend_all, finish, h_drain = drift_tools(
+    slots, publish, relay, arrive, keys_values, queries, attend, attend_all, finish, h_drain = drift_tools(
         PIECES, p, dp, mask, g1, g2, nb, wq, wk, wv, wo, wu, wd, kb, vb, qb, mb, att, h_send, h_recv
     )
 
@@ -574,20 +574,22 @@
     for t in range(now, STEPS):
         step(t)
 
-    for h in range(HEADS):
-        attend_all(h)
-
-    first[...] = finish(st)
-    for c in range(PIECES):
-        t = STEPS - PIECES + c
-        if t >= STEPS - LAG:
-            for way in range(2):
-                take(t, way)
-        part = pl.ds(c * rows, rows)
-        base = st[part].astype(F32) + 0.3 * piece(1, c).astype(F32)
-        x = (base + 0.5 * first[part].astype(F32)).astype(BF)
-        fx[part] = x
-        publish(1, c, x)
+    blocks = nodes // BLOCK
+    for b in range(blocks):
+        for h in range(HEADS):
+            attend(b, h)
+        half = pl.ds(b * BLOCK, BLOCK)
+        first[half] = finish(st, half)
+        for c in range(b * PIECES // blocks, (b + 1) * PIECES // blocks):
+            t = STEPS - PIECES + c
+            if t >= STEPS - LAG:
+                for way in range(2):
+                    take(t, way)
+            part = pl.ds(c * rows, rows)
+            base = st[part].astype(F32) + 0.3 * piece(1, c).astype(F32)
+            x = (base + 0.5 * first[part].astype(F32)).astype(BF)
+            fx[part] = x
+            publish(1, c, x)
     queries(1)
     keys_values(1, 2)
     for c in range(PIECES // 2):

time: 90.7 us -> 90.1 us (level)
  no operation moved by 1% of the time
where the time goes in v5:
time: 90.1 us; the launch traced here: 89.9 us
  Pallas kernels  87.2 us (97%)
  local copies, waits for them, and re-layouts  2 us (2%)
    pallas_call x1, Pallas kernels, shards(): pl.pallas_call(functools.partial(route_kernel, members, patches), out_sha...  87.2 us
    unnamed x27, local copies, waits for them, and re-layouts  2 us

profile of v5, /device:TPU:1, one launch (start us, length us, event | category | flops | bytes accessed | tf_op | source)
XLA Modules:
  0.0 89.9 jit_solution(8808314882722184958)
XLA Ops:
  0.0 0.0 copy-start.9
  0.0 0.0 copy-start.8
  0.0 0.0 copy-start.10
  0.0 0.0 copy-start.11
  0.0 0.7 copy-done.9
  0.7 0.0 copy-done.8
  0.7 0.0 copy-done.10
  0.7 0.0 copy-done.11
  0.7 0.0 copy-start
  0.7 0.0 copy-start.1
  0.7 0.0 copy-start.2
  0.7 0.0 copy-start.3
  0.7 0.0 copy-start.4
  0.7 0.0 copy-start.5
  0.8 0.0 copy-start.6
  0.8 0.0 copy-start.7
  0.8 87.2 %route.1 = (bf16[1,256,512]{2,1,0:T(8,128)(2,1)S(1)}, s32[1,1]{1,0:T(1,128)}) custom-call(s32[16]{0:T(128)S(1)} %copy-done.11, s32[16]{0:T(128)} %refs_1_.1, s32[2,8]{1,0:T(2,128)S(1)} %copy-done.10, bf16[1,256,512]{2,1,0:T(8,128)(2,1)} %refs_3_.1, bf16[1,256,512]{2,1,0:T(8,128)(2,1)} %refs_4_.1, f32[1,512]{1,0:T(1,128)S(1)} %bitcast.3, ...), custom_call_target="tpu_custom_call" | custom-call | tf_op jit(solution)/shard_map/route/pallas_call | solution.py:659
  88.6 0.0 copy-start.12
  88.6 0.0 copy-done
  88.6 0.0 copy-done.1
  88.6 0.0 copy-done.2
  88.6 0.0 copy-done.3
  88.6 0.0 copy-done.4
  88.6 0.0 copy-done.5
  88.7 0.0 copy-done.6
  88.7 0.0 copy-done.7
  88.7 0.6 copy-done.12
  89.2 0.7 copy.19
  (1 shorter events, 0.0 us)
Async XLA Ops:
  0.0 0.7 copy-start.9
  0.0 0.7 copy-start.8
  0.0 0.7 copy-start.10
  0.0 0.7 copy-start.11
  0.7 87.9 %copy-start = (bf16[512,1024]{1,0:T(8,128)(2,1)S(1)}, bf16[512,1024]{1,0:T(8,128)(2,1)}, u32[]{:S(2)}) copy-start(bf16[512,1024]{1,0:T(8,128)(2,1)} %refs_11_.1) | copy-start | bytes 3145732
  0.7 87.9 %copy-start.1 = (bf16[1024,512]{1,0:T(8,128)(2,1)S(1)}, bf16[1024,512]{1,0:T(8,128)(2,1)}, u32[]{:S(2)}) copy-start(bf16[1024,512]{1,0:T(8,128)(2,1)} %refs_12_.1) | copy-start | bytes 3145732
  0.7 87.9 %copy-start.2 = (bf16[512,512]{1,0:T(8,128)(2,1)S(1)}, bf16[512,512]{1,0:T(8,128)(2,1)}, u32[]{:S(2)}) copy-start(bf16[512,512]{1,0:T(8,128)(2,1)} %refs_7_.1) | copy-start | bytes 1572868
  0.7 87.9 %copy-start.3 = (bf16[512,512]{1,0:T(8,128)(2,1)S(1)}, bf16[512,512]{1,0:T(8,128)(2,1)}, u32[]{:S(2)}) copy-start(bf16[512,512]{1,0:T(8,128)(2,1)} %refs_8_.1) | copy-start | bytes 1572868
  0.7 87.9 %copy-start.4 = (bf16[512,512]{1,0:T(8,128)(2,1)S(1)}, bf16[512,512]{1,0:T(8,128)(2,1)}, u32[]{:S(2)}) copy-start(bf16[512,512]{1,0:T(8,128)(2,1)} %refs_9_.1) | copy-start | bytes 1572868
  0.7 87.9 %copy-start.5 = (bf16[512,512]{1,0:T(8,128)(2,1)S(1)}, bf16[512,512]{1,0:T(8,128)(2,1)}, u32[]{:S(2)}) copy-start(bf16[512,512]{1,0:T(8,128)(2,1)} %refs_10_.1) | copy-start | bytes 1572868
  0.8 87.9 %copy-start.6 = (bf16[1,256,512]{2,1,0:T(8,128)(2,1)S(1)}, bf16[1,256,512]{2,1,0:T(8,128)(2,1)}, u32[]{:S(2)}) copy-start(bf16[1,256,512]{2,1,0:T(8,128)(2,1)} %refs_3_.1) | copy-start | bytes 786436
  0.8 87.9 %copy-start.7 = (bf16[1,256,512]{2,1,0:T(8,128)(2,1)S(1)}, bf16[1,256,512]{2,1,0:T(8,128)(2,1)}, u32[]{:S(2)}) copy-start(bf16[1,256,512]{2,1,0:T(8,128)(2,1)} %refs_4_.1) | copy-start | bytes 786436
  88.6 0.7 copy-start.12
